TPU v7x, 512 devices: a whole 4x8x8 slice. The times are simulated.
512 devices in a mesh: sat: 16 (over z, core), seg: 32 (over y, x).
Axes of the slice: x: 4, y: 8, z: 8, core: 2. Of those that a mesh axis runs over, the one named last changes fastest.
Arguments:
- sens_params: bfloat16 [16, 32, 320, 1024], P('sat', 'seg'), may hold values from -0.59765625 to 0.59765625
- sens_state: bfloat16 [16, 32, 320, 64], P('sat', 'seg'), may hold values from -0.59765625 to 0.59765625
- misfit: float32 [16, 32, 320], P('sat', 'seg'), may hold values from -6 to 6
- depth: float32 [16, 32, 320], P('sat', 'seg'), may hold values from 0.2 to 0.9
- cycle_count: int32 [16, 32], P('sat', 'seg'), may hold values from 80 to 320, as said below
- node_side: int32 [16, 32, 320], P('sat', 'seg'), may hold values from 0 to 1, as said below
- transition: bfloat16 [16, 32, 64, 64], P('sat', 'seg'), may hold values from -0.75 to 0.75
- cont_sens: bfloat16 [16, 32, 64, 1024], P('sat', 'seg'), may hold values from -0.59765625 to 0.59765625
- noise_root: float32 [16, 32, 64, 64], P('sat', 'seg'), may hold values from -0.4 to 0.4
- cont_misfit: float32 [16, 32, 64], P('sat', 'seg'), may hold values from -6 to 6
Outputs:
- gram_params: float32 [1024, 1024], P('sat')
- grad_params: float32 [1024], replicated
- node_hess: float32 [16, 32, 64, 64], P('sat', 'seg')
- node_cross: float32 [16, 32, 64, 1024], P('sat', 'seg')
- node_grad: float32 [16, 32, 64], P('sat', 'seg')
- node_coupling: float32 [16, 32, 64, 64], P('sat', 'seg')
Inputs may be any that keep to these rules, and one draw needn't show every extreme that they name: `cycle_count`: in every segment some satellite has exactly 320 cycles. `node_side`: along the cycles of one satellite's segment the value never falls, and both values occur.
All inputs are finite; a program needn't handle non-finite values.
Results may differ from a plain program's by a relative error of at most 0.0015.
The roundings to bfloat16 on the way count: a program that leaves them out, or rounds other values in their place, can miss the bound.
Values sent between devices are 32-bit elements; how exact they have to be, the bound alone decides.
A program may use at most 64 MiB of HBM per device.

v0:
```python
import jax
import jax.numpy as jnp
from jax import lax
from jax.sharding import PartitionSpec as P

highest = lax.Precision.HIGHEST


def entering(value, axis, combine, identity):
    devices, position = (lax.axis_size(axis), lax.axis_index(axis))
    everything = lax.all_gather(value, axis)
    start = jnp.broadcast_to(jnp.asarray(identity, value.dtype), value.shape)

    def step(k, before):
        reached = k < position
        new = combine(before, everything[k])
        return jnp.where(reached, new, before)

    return lax.fori_loop(0, devices, step, start)


def passed_along(block, axis, distance):
    devices = range(lax.axis_size(axis))
    route = [(i - distance, i) for i in devices if i - distance in devices]
    return lax.ppermute(block, axis, route)


def add_pair(earlier, later):
    return earlier + later


def shards(
    sens_params,
    sens_state,
    misfit,
    depth,
    cycle_count,
    node_side,
    transition,
    cont_sens,
    noise_root,
    cont_misfit,
):
    sat_dev = sens_params.shape[0]
    cycles = sens_params.shape[2]
    params = sens_params.shape[3]
    states = sens_state.shape[3]
    sat_count = lax.axis_size("sat")
    seg_count = lax.axis_size("seg")
    seg_place = lax.axis_index("seg")
    positions = jnp.arange(cycles, dtype=jnp.int32)
    live_mask = (positions[None, :] < cycle_count).astype(jnp.float32)
    used_depth = live_mask * depth[:, 0]
    through = jnp.sum(used_depth, axis=1)
    prior_age = entering(through, "seg", add_pair, jnp.zeros_like(through))
    upper_tri = (positions[:, None] < positions[None, :]).astype(jnp.float32)
    inner_age = jnp.dot(used_depth, upper_tri, precision=highest)
    age_scale = 4.0 / (cycles * seg_count)
    weights = live_mask / (1.0 + (prior_age[:, None] + inner_age) * age_scale)
    root_seg = jnp.sqrt(weights)
    weighted_sens = (root_seg[:, :, None] * sens_params[:, 0]).astype(jnp.bfloat16)
    weighted_res = (root_seg * misfit[:, 0]).astype(jnp.bfloat16)
    side = node_side[:, 0].astype(jnp.float32)[:, :, None]
    state_rows = root_seg[:, :, None] * sens_state[:, 0]
    state_pair = jnp.concatenate([state_rows * (1.0 - side), state_rows * side], axis=2).astype(
        jnp.bfloat16
    )
    live_link = (seg_place < seg_count - 1).astype(jnp.float32)
    eye_block = jnp.eye(states, dtype=jnp.float32)
    root_info = (eye_block[None] + noise_root[:, 0]) * live_link
    state_map = jnp.einsum(
        "sab,sbc->sac", root_info, transition[:, 0].astype(jnp.float32), precision=highest
    )
    param_map = jnp.einsum(
        "sab,sbp->sap", root_info, cont_sens[:, 0].astype(jnp.float32), precision=highest
    ).astype(jnp.bfloat16)
    cont_res = jnp.einsum("sab,sb->sa", root_info, cont_misfit[:, 0], precision=highest).astype(
        jnp.bfloat16
    )
    stacked = jnp.concatenate([weighted_sens, param_map], axis=1).reshape(-1, params)
    res_vec = jnp.concatenate([weighted_res, -cont_res], axis=1).reshape(-1)
    norm_factor = 1.0 / (sat_dev * sat_count * seg_count)
    term = lax.dot_general(
        stacked, stacked, (((0,), (0,)), ((), ())), preferred_element_type=jnp.float32
    )
    row_block = lax.psum_scatter(
        term * norm_factor, ("sat", "seg"), scatter_dimension=0, tiled=True
    )
    gram_params = lax.all_gather(row_block, "seg", axis=0, tiled=True)
    grad_term = jnp.dot(res_vec, stacked, preferred_element_type=jnp.float32) * norm_factor
    grad_params = lax.psum(grad_term, ("sat", "seg"))
    pair_gram = jnp.einsum(
        "smi,smk->sik", state_pair, state_pair, preferred_element_type=jnp.float32
    )
    pair_cross = jnp.einsum(
        "smi,smp->sip", state_pair, weighted_sens, preferred_element_type=jnp.float32
    )
    pair_grad = jnp.einsum(
        "smi,sm->si", state_pair, weighted_res, preferred_element_type=jnp.float32
    )
    map_float = param_map.astype(jnp.float32)
    res_float = cont_res.astype(jnp.float32)
    own_hess = pair_gram[:, :states, :states] + jnp.einsum(
        "sai,saj->sij", state_map, state_map, precision=highest
    )
    own_cross = pair_cross[:, :states] + jnp.einsum(
        "sai,sap->sip", state_map, map_float, precision=highest
    )
    own_grad = pair_grad[:, :states] - jnp.einsum(
        "sai,sa->si", state_map, res_float, precision=highest
    )
    next_hess = pair_gram[:, states:, states:] + jnp.einsum(
        "sai,saj->sij", root_info, root_info, precision=highest
    )
    next_cross = pair_cross[:, states:] - jnp.einsum(
        "sai,sap->sip", root_info, map_float, precision=highest
    )
    next_grad = pair_grad[:, states:] + jnp.einsum(
        "sai,sa->si", root_info, res_float, precision=highest
    )
    coupling = -jnp.einsum("sai,saj->sij", state_map, root_info, precision=highest)
    got_hess, got_cross, got_grad = passed_along((next_hess, next_cross, next_grad), "seg", 1)
    node_hess = (own_hess + got_hess)[:, None]
    node_cross = (own_cross + got_cross)[:, None]
    node_grad = (own_grad + got_grad)[:, None]
    node_coupling = coupling[:, None]
    return (gram_params, grad_params, node_hess, node_cross, node_grad, node_coupling)


def solution(mesh):
    placed = (
        P("sat", "seg", None, None),
        P("sat", "seg", None, None),
        P("sat", "seg", None),
        P("sat", "seg", None),
        P("sat", "seg"),
        P("sat", "seg", None),
        P("sat", "seg", None, None),
        P("sat", "seg", None, None),
        P("sat", "seg", None, None),
        P("sat", "seg", None),
    )
    return jax.shard_map(
        shards,
        mesh=mesh,
        in_specs=placed,
        out_specs=(
            P("sat", None),
            P(),
            P("sat", "seg", None, None),
            P("sat", "seg", None, None),
            P("sat", "seg", None),
            P("sat", "seg", None, None),
        ),
        check_vma=False,
    )
```

profile of v0, /device:TPU:16, one launch (start us, length us, event | category | flops | bytes accessed | tf_op | source)
XLA Modules:
  0.0 479.6 jit_solution(1217586959932746977)
XLA Ops:
  7.9 1.3 fusion.38
  9.2 1.3 dynamic-slice
  10.5 1.4 dynamic-update-slice
  11.9 63.0 %all-reduce = f32[32]{0:T(128)S(1)} all-reduce(f32[32]{0:T(128)S(1)} %dynamic-update-slice), channel_id=1, replica_groups=mesh['sat'=16,'seg'=32] {'seg'}, use_global_device_ids=true, to_apply=%add | all-reduce | flops 32 | bytes 256
  74.8 40.4 %while.13 = (s32[]{:T(128)}, f32[1]{0:T(128)}, s32[]{:T(128)}, f32[32,1]{0,1:T(1,128)S(1)}, s32[]{:T(128)}) while((s32[]{:T(128)}, f32[1]{0:T(128)}, s32[]{:T(128)}, f32[32,1]{0,1:T(1,128)S(1)}, s32[]{:T(128)}) %tuple.40), condition=%wide.region_2.3_spmd, body=%wide.region_1.2_spmd.sunk | while | flops 5 | bytes 115 | solution.py:19
  76.1 0.6 constant_dynamic-slice_fusion.2
  115.2 0.7 convert_reduce_fusion
  115.9 0.7 reduce.1
  116.6 0.7 reduce.3
  117.6 1.3 fusion.1
  119.2 3.3 convolution_multiply_fusion
  122.4 0.6 copy-done.5
  123.5 3.7 collective-permute-start.2
  127.6 3.1 collective-permute-start
  131.5 4.6 collective-permute-start.1
  136.5 0.9 fusion.8
  137.3 110.4 %psum.7 = f32[1024]{0:T(1024)} all-reduce(f32[1024]{0:T(1024)S(1)} %broadcast_multiply_fusion), channel_id=1, replica_groups=mesh['sat'=16,'seg'=32] {'sat','seg'}, use_global_device_ids=true, to_apply=%region_4.5 | all-reduce | flops 1024 | bytes 8192 | tf_op jit(solution)/shard_map/psum | solution.py:91
  247.8 0.7 fusion.15
  248.4 0.9 fusion.11
  249.3 1.0 fusion.6
  250.3 171.4 %all-reduce.4.cloned.1.call-done = f32[1024,1024]{1,0:T(8,128)} async-done(((f32[1024,1024]{1,0:T(8,128)}), f32[1024,1024]{1,0:T(8,128)}) %all-reduce.4.cloned.1.call-update) | async-done | bytes 4194320
  421.8 0.8 dynamic-slice_bitcast_fusion
  422.5 49.4 %all-gather = f32[32,2,1024]{2,1,0:T(2,128)S(1)} all-gather(f32[1,2,1024]{2,1,0:T(2,128)S(1)} %dynamic-slice_bitcast_fusion), channel_id=1, replica_groups=mesh['sat'=16,'seg'=32] {'seg'}, dimensions={0}, use_global_device_ids=true | all-gather | bytes 270336 | tf_op jit(solution)/shard_map/all_gather | solution.py:89
  471.9 0.9 reshape.312
  (67 shorter events, 20.7 us)
Async XLA Ops:
  7.2 111.7 %copy-start = (bf16[1,1,64,1024]{3,2,1,0:T(8,128)(2,1)S(1)}, bf16[1,1,64,1024]{3,2,1,0:T(8,128)(2,1)}, u32[]{:S(2)}) copy-start(bf16[1,1,64,1024]{3,2,1,0:T(8,128)(2,1)} %param.19) | copy-start | bytes 393220
  7.2 111.7 %copy-start.2 = (f32[1,1,64,64]{3,2,1,0:T(8,128)S(1)}, f32[1,1,64,64]{3,2,1,0:T(8,128)}, u32[]{:S(2)}) copy-start(f32[1,1,64,64]{3,2,1,0:T(8,128)} %param.20) | copy-start | bytes 49156
  7.2 414.6 %all-reduce.4.cloned.1.call-start = ((), (), s32[]{:S(2)}) async-start(), calls=%async_computation | async-start | bytes 8388608
  122.4 0.7 copy-start.5
  122.4 0.8 copy-start.3
  122.4 8.4 %copy-start.1 = (bf16[1,1,320,1024]{3,2,1,0:T(8,128)(2,1)S(1)}, bf16[1,1,320,1024]{3,2,1,0:T(8,128)(2,1)}, u32[]{:S(2)}) copy-start(bf16[1,1,320,1024]{3,2,1,0:T(8,128)(2,1)} %param.12) | copy-start | bytes 1966084
  123.5 124.3 %collective-permute-start.2 = (f32[1,64]{1,0:T(1,128)S(1)}, f32[1,64]{1,0:T(1,128)S(1)}, u32[]{:S(2)}, u32[]{:S(2)}) collective-permute-start(f32[1,64]{1,0:T(1,128)S(1)} %convolution_add_fusion), channel_id=1, source_target_pairs={{0,1},{1,2},{2,3},{3,4},{4,5},{5,6},{6,7},{7,8},{8,9},{9,10},{10,1... | collective-permute-start | bytes 776 | tf_op jit(solution)/shard_map/ppermute | solution.py:25
  127.6 8.7 %copy-start.4 = (bf16[1,1,64,64]{3,2,1,0:T(8,128)(2,1)S(1)}, bf16[1,1,64,64]{3,2,1,0:T(8,128)(2,1)}, u32[]{:S(2)}) copy-start(bf16[1,1,64,64]{3,2,1,0:T(8,128)(2,1)} %param.18) | copy-start | bytes 24580
  127.6 120.8 %collective-permute-start = (f32[1,64,64]{2,1,0:T(8,128)S(1)}, f32[1,64,64]{2,1,0:T(8,128)S(1)}, u32[]{:S(2)}, u32[]{:S(2)}) collective-permute-start(f32[1,64,64]{2,1,0:T(8,128)S(1)} %fusion.12), channel_id=1, source_target_pairs={{0,1},{1,2},{2,3},{3,4},{4,5},{5,6},{6,7},{7,8},{8,9},{9,10},{10,1... | collective-permute-start | bytes 49160 | tf_op jit(solution)/shard_map/ppermute | solution.py:25
  131.5 117.8 %collective-permute-start.1 = (f32[1,64,1024]{2,1,0:T(8,128)S(1)}, f32[1,64,1024]{2,1,0:T(8,128)S(1)}, u32[]{:S(2)}, u32[]{:S(2)}) collective-permute-start(f32[1,64,1024]{2,1,0:T(8,128)S(1)} %fusion.7), channel_id=1, source_target_pairs={{0,1},{1,2},{2,3},{3,4},{4,5},{5,6},{6,7},{7,8},{8,9},{9,10},{10,1... | collective-permute-start | bytes 786440 | tf_op jit(solution)/shard_map/ppermute | solution.py:25
Sparse Core Ops, SparseCore 0:
  122.6 299.1 all-reduce.3
where the time goes:
time: 481 us; the launch traced here: 480 us
  blocking collectives  223 us (46%)
  waiting for transfers between devices  171 us (36%)
  local copies, waits for them, and re-layouts  23.7 us (5%)
  loops' own time  21.7 us (5%)
  between operations  14.9 us (3%)
  starting transfers between devices  11.4 us (2%)
  matrix products  9.03 us (2%)
    unnamed x2, waiting for transfers between devices  171 us
    psum x1, blocking collectives, shards(): grad_params = lax.psum(grad_term, ('sat', 'seg'))  110 us
    unnamed x1, blocking collectives  63 us
    all_gather x1, blocking collectives, shards(): gram_params = lax.all_gather(row_block, 'seg', axis=0, tiled=True)  49.4 us
    another operation x1, loops' own time, entering(): return lax.fori_loop(0, devices, step, start)  21.7 us
    dynamic_slice x32, local copies, waits for them, and re-layouts, step(): new = combine(before, everything[k])  18.7 us
    ppermute x3, starting transfers between devices, passed_along(): return lax.ppermute(block, axis, route)  11.3 us
  transfers between devices with their start and end apart: 4, of which 1 were waited for; matrix products, arithmetic and copies ran while one was open for 1% of the time, Pallas kernels for 0%

commit v1 on v0

v1 whole, which is shorter than its diff:
```python
import jax
import jax.numpy as jnp
from jax import lax
from jax.experimental import pallas as pl
from jax.experimental.pallas import tpu as pltpu
from jax.sharding import PartitionSpec as P

highest = lax.Precision.HIGHEST
MESH = pl.DeviceIdType.MESH
F32 = jnp.float32
BF16 = jnp.bfloat16

NX, NY, NZ = 4, 8, 8
M, S, PS = 320, 64, 1024
COLS = PS // NX
HALF = NZ // 2 * 64


def dot0(a, b, precision=None):
    return lax.dot_general(
        a, b, (((0,), (0,)), ((), ())), precision=precision, preferred_element_type=F32
    )


def kernel(
    sp, ss, mis, dep, cc, side, tr, cs, nr, cm,
    gram, grad, hess, cross, ngrad, coup,
    A, G2, R0, RX1, RX2, W, RY, V, RZ, FIN,
    TX, TY, GC, GX, GY, GZ, HB, HC, HBr, HCr,
    tx_s, tx_r, ty_s, ty_r, core_s, core_r, x1_s, x1_r, x2_s, x2_r,
    y_s, y_r, z_s, z_r, ay_s, ay_r, ax_s, ax_r,
    gc_s, gc_r, gx_s, gx_r, gy_s, gy_r, gz_s, gz_r, h_s, h_r,
):
    sat = lax.axis_index("sat")
    seg = lax.axis_index("seg")
    z, c = sat // 2, sat % 2
    y, x = seg // NX, seg % NX

    core_dev = (sat + 1 - 2 * c, seg)

    def x_dev(k):
        return (sat, y * NX + (x + k) % NX)

    def y_dev(k):
        return (sat, ((y + k) % NY) * NX + x)

    def z_dev(k):
        return (((z + k) % NZ) * 2 + c, seg)

    after = (sat, (seg + 1) % (NX * NY))
    before = (sat, (seg + NX * NY - 1) % (NX * NY))

    def copy(src, dst, send, recv, dev):
        return pltpu.make_async_remote_copy(
            src_ref=src, dst_ref=dst, send_sem=send, recv_sem=recv,
            device_id=dev, device_id_type=MESH,
        )

    barrier = pltpu.get_barrier_semaphore()
    partners = [core_dev, after, before]
    partners += [x_dev(k) for k in range(1, NX)]
    partners += [y_dev(k) for k in range(1, NY)]
    partners += [z_dev(k) for k in range(1, NZ)]
    for dev in partners:
        pl.semaphore_signal(barrier, inc=1, device_id=dev, device_id_type=MESH)

    rows = lax.broadcasted_iota(jnp.int32, (M, M), 0)
    lanes = lax.broadcasted_iota(jnp.int32, (M, M), 1)
    count = cc[...]
    used = jnp.where(lax.broadcasted_iota(jnp.int32, (1, M), 1) < count, dep[...], 0.0)
    through = jnp.sum(used, axis=1, keepdims=True)
    TX[x] = jnp.broadcast_to(through, (1, 128))

    pl.semaphore_wait(barrier, len(partners))

    def tx(k):
        return copy(TX.at[x], TX.at[x], tx_s.at[k - 1], tx_r.at[k - 1], x_dev(k))

    for k in range(1, NX):
        tx(k).start()

    link = jnp.where(seg < NX * NY - 1, 1.0, 0.0).astype(F32)
    r64 = lax.broadcasted_iota(jnp.int32, (S, S), 0)
    l64 = lax.broadcasted_iota(jnp.int32, (S, S), 1)
    root = (jnp.where(r64 == l64, 1.0, 0.0) + nr[...]) * link
    pm = jnp.dot(
        root, cs[...].astype(F32), precision=highest, preferred_element_type=F32
    ).astype(BF16)
    A[M:, :] = pm
    inner = jnp.sum(jnp.where(lanes < rows, used, 0.0), axis=1, keepdims=True)

    for k in range(1, NX):
        tx(k).wait_recv()
    xprior = jnp.zeros((1, 128), F32)
    total = jnp.zeros((1, 128), F32)
    for k in range(NX):
        part = TX[k]
        total = total + part
        xprior = xprior + jnp.where(k < x, part, 0.0)
    TY[y] = total

    def ty(k):
        return copy(TY.at[y], TY.at[y], ty_s.at[k - 1], ty_r.at[k - 1], y_dev(k))

    for k in range(1, NY):
        ty(k).start()

    smap = jnp.dot(
        root, tr[...].astype(F32), precision=highest, preferred_element_type=F32
    )
    both = jnp.concatenate([smap, root], axis=1)
    small = dot0(both, both, highest)
    wide = dot0(both, pm.astype(F32), highest)
    coup[...] = -small[:S, S:]
    cres = jnp.sum(root * cm[...], axis=1, keepdims=True).astype(BF16).astype(F32)
    cres_row = jnp.sum(jnp.where(r64 == l64, cres, 0.0), axis=0, keepdims=True)
    state_grad = jnp.sum(both * cres, axis=0, keepdims=True)
    side_f = side[...].astype(F32)
    side_col = jnp.sum(jnp.where(rows == lanes, side_f, 0.0), axis=1, keepdims=True)
    live_col = jnp.where(
        lax.broadcasted_iota(jnp.int32, (M, 1), 0) < count, 1.0, 0.0
    ).astype(F32)

    for k in range(1, NY):
        ty(k).wait_recv()
    prior = xprior
    for k in range(NY):
        prior = prior + jnp.where(k < y, TY[k], 0.0)

    age = inner + prior[:, 0:1]
    weight = jnp.sqrt(live_col / (1.0 + age * (4.0 / (M * NX * NY))))
    weight_row = jnp.sum(jnp.where(rows == lanes, weight, 0.0), axis=0, keepdims=True)
    A[:M, :] = (weight * sp[...].astype(F32)).astype(BF16)
    state_rows = weight * ss[...].astype(F32)
    pair = jnp.concatenate(
        [state_rows * (1.0 - side_col), state_rows * side_col], axis=1
    ).astype(BF16)
    res8 = jnp.broadcast_to(weight_row * mis[...], (8, M)).astype(BF16)
    cres8 = jnp.broadcast_to(cres_row, (8, S)).astype(BF16)
    ws = A[:M, :]

    pgram = dot0(pair, pair)
    pcross = dot0(pair, ws)
    pgrad = jnp.dot(res8, pair, preferred_element_type=F32)[0:1]
    HC[...] = pcross[S:] - wide[S:]
    HB[...] = jnp.zeros_like(HB)
    HB[0:S, 0:S] = pgram[S:, S:] + small[S:, S:]
    HB[S : S + 1, 0:S] = pgrad[:, S:] + state_grad[:, S:]

    halo = [
        copy(HC, HCr, h_s.at[0], h_r.at[0], after),
        copy(HB, HBr, h_s.at[1], h_r.at[1], after),
    ]

    @pl.when(seg < NX * NY - 1)
    def _():
        for h in halo:
            h.start()

    cross[...] = pcross[:S] + wide[:S]
    hess[...] = pgram[:S, :S] + small[:S, :S]
    ngrad[...] = pgrad[:, :S] - state_grad[:, :S]

    def core_copy(zi):
        part = pl.ds(pl.multiple_of(zi * 64, 64), 64)
        return copy(
            G2.at[1 - c, :, part, :], R0.at[:, part, :], core_s.at[zi], core_r.at[zi], core_dev
        )

    def gram_step(i, _):
        zi = (i % 2) * (NZ // 2) + i // 2
        g = dot0(A[:, pl.ds(pl.multiple_of(zi * 128, 128), 128)], A[...])
        part = pl.ds(pl.multiple_of(zi * 64, 64), 64)
        for q in range(NX):
            G2[0, q, part, :] = g[:64, q * COLS : (q + 1) * COLS]
            G2[1, q, part, :] = g[64:, q * COLS : (q + 1) * COLS]
        core_copy(zi).start()
        return 0

    lax.fori_loop(0, NZ, gram_step, 0)

    GC[0] = (
        jnp.dot(res8, ws, preferred_element_type=F32)
        - jnp.dot(cres8, pm, preferred_element_type=F32)
    )[0:1]
    gc = copy(GC.at[0], GC.at[1], gc_s, gc_r, core_dev)
    gc.start()

    far, right, left = (x + 2) % NX, (x + 1) % NX, (x + 3) % NX

    def rows64(j):
        return pl.ds(pl.multiple_of(j * 64, 64), 64)

    def x1(d, j):
        zi = d * (NZ // 2) + j
        return copy(
            R0.at[far, rows64(zi), :], RX1.at[d, rows64(j), :],
            x1_s.at[d, j], x1_r.at[d, j], x_dev(1 if d == 0 else 3),
        )

    def x2(d, zi):
        return copy(
            R0.at[right if d == 0 else left, rows64(zi), :], RX2.at[d, rows64(zi), :],
            x2_s.at[d, zi], x2_r.at[d, zi], x_dev(1 if d == 0 else 3),
        )

    def x_first(j, _):
        for d in range(2):
            zi = d * (NZ // 2) + j
            core_copy(zi).wait_recv()
            R0[:, rows64(zi), :] = R0[:, rows64(zi), :] + G2[c, :, rows64(zi), :]
            x1(d, j).start()
        for d in range(2):
            x2(1 - d, d * (NZ // 2) + j).start()
        return 0

    lax.fori_loop(0, NZ // 2, x_first, 0)

    gc.wait_recv()
    GX[x] = GC[0] + GC[1]

    def gx(k):
        return copy(GX.at[x], GX.at[x], gx_s.at[k - 1], gx_r.at[k - 1], x_dev(k))

    for k in range(1, NX):
        gx(k).start()

    def x_second(j, _):
        for d in range(2):
            zi = d * (NZ // 2) + j
            dest = right if d == 0 else left
            x1(d, j).wait_recv()
            R0[dest, rows64(zi), :] = R0[dest, rows64(zi), :] + RX1[d, rows64(j), :]
            x2(d, zi).start()
        return 0

    lax.fori_loop(0, NZ // 2, x_second, 0)

    for k in range(1, NX):
        gx(k).wait_recv()
    GY[y] = (GX[0] + GX[1]) + (GX[2] + GX[3])

    def gy(k):
        return copy(GY.at[y], GY.at[y], gy_s.at[k - 1], gy_r.at[k - 1], y_dev(k))

    for k in range(1, NY):
        gy(k).start()

    def x_last(i, _):
        zi = (i % 2) * (NZ // 2) + i // 2
        for d in range(2):
            x2(d, zi).wait_recv()
        own = R0[x, rows64(zi), :] + RX2[0, rows64(zi), :] + RX2[1, rows64(zi), :]
        W[:, zi] = own.reshape(NY, 8, COLS)
        return 0

    lax.fori_loop(0, NZ, x_last, 0)

    def yc(k):
        return copy(W.at[(y + k) % NY], RY.at[k - 1], y_s.at[k - 1], y_r.at[k - 1], y_dev(k))

    for k in range(1, NY):
        yc(k).start()
    for k in range(1, NY):
        gy(k).wait_recv()
    part = GY[0]
    for k in range(1, NY):
        part = part + GY[k]
    GZ[z] = part

    def gz(k):
        return copy(GZ.at[z], GZ.at[z], gz_s.at[k - 1], gz_r.at[k - 1], z_dev(k))

    for k in range(1, NZ):
        gz(k).start()

    @pl.when(seg > 0)
    def _():
        for h in halo:
            h.wait_recv()
        cross[...] = cross[...] + HCr[...]
        hess[...] = hess[...] + HBr[0:S, 0:S]
        ngrad[...] = ngrad[...] + HBr[S : S + 1, 0:S]

    V[...] = W[y]
    for k in range(1, NY):
        yc(k).wait_recv()
        V[...] = V[...] + RY[k - 1]

    def zc(k):
        return copy(V.at[(z + k) % NZ], RZ.at[k - 1], z_s.at[k - 1], z_r.at[k - 1], z_dev(k))

    for k in range(1, NZ):
        zc(k).start()
    for k in range(1, NZ):
        gz(k).wait_recv()
    part = GZ[0]
    for k in range(1, NZ):
        part = part + GZ[k]
    scale = 1.0 / (2 * NX * NY * NZ)
    grad[...] = part * scale

    own = V[z]
    for k in range(1, NZ):
        zc(k).wait_recv()
        own = own + RZ[k - 1]
    FIN[x, y] = own * scale

    def ay(k):
        return copy(FIN.at[x, y], FIN.at[x, y], ay_s.at[k - 1], ay_r.at[k - 1], y_dev(k))

    for k in range(1, NY):
        ay(k).start()
    for k in range(1, NY):
        ay(k).wait_recv()

    def ax(k):
        return copy(FIN.at[x], FIN.at[x], ax_s.at[k - 1], ax_r.at[k - 1], x_dev(k))

    for k in range(1, NX):
        ax(k).start()
    for k in range(1, NX):
        ax(k).wait_recv()
    for q in range(NX):
        gram[:, q * COLS : (q + 1) * COLS] = FIN[q].reshape(64, COLS)

    for k in range(1, NX):
        tx(k).wait_send()
        gx(k).wait_send()
        ax(k).wait_send()
    for k in range(1, NY):
        ty(k).wait_send()
        gy(k).wait_send()
        yc(k).wait_send()
        ay(k).wait_send()
    for k in range(1, NZ):
        gz(k).wait_send()
        zc(k).wait_send()
    gc.wait_send()

    def drain(zi, _):
        core_copy(zi).wait_send()
        for d in range(2):
            x2(d, zi).wait_send()
        return 0

    lax.fori_loop(0, NZ, drain, 0)

    def drain1(j, _):
        for d in range(2):
            x1(d, j).wait_send()
        return 0

    lax.fori_loop(0, NZ // 2, drain1, 0)

    @pl.when(seg < NX * NY - 1)
    def _():
        for h in halo:
            h.wait_send()


def shards(sp, ss, mis, dep, cc, side, tr, cs, nr, cm):
    vmem = pl.BlockSpec(memory_space=pltpu.VMEM)
    sem = pltpu.SemaphoreType.DMA
    shapes = [(64, PS), (1, PS), (S, S), (S, PS), (1, S), (S, S)]
    outs = pl.pallas_call(
        kernel,
        out_shape=[jax.ShapeDtypeStruct(s, F32) for s in shapes],
        in_specs=[vmem] * 10,
        out_specs=[vmem] * 6,
        scratch_shapes=[
            pltpu.VMEM((M + S, PS), BF16),
            pltpu.VMEM((2, NX, 512, COLS), F32),
            pltpu.VMEM((NX, 512, COLS), F32),
            pltpu.VMEM((2, HALF, COLS), F32),
            pltpu.VMEM((2, 512, COLS), F32),
            pltpu.VMEM((NY, NZ, 8, COLS), F32),
            pltpu.VMEM((NY - 1, NZ, 8, COLS), F32),
            pltpu.VMEM((NZ, 8, COLS), F32),
            pltpu.VMEM((NZ - 1, 8, COLS), F32),
            pltpu.VMEM((NX, NY, 8, COLS), F32),
            pltpu.VMEM((NX, 1, 128), F32),
            pltpu.VMEM((NY, 1, 128), F32),
            pltpu.VMEM((2, 1, PS), F32),
            pltpu.VMEM((NX, 1, PS), F32),
            pltpu.VMEM((NY, 1, PS), F32),
            pltpu.VMEM((NZ, 1, PS), F32),
            pltpu.VMEM((72, 128), F32),
            pltpu.VMEM((S, PS), F32),
            pltpu.VMEM((72, 128), F32),
            pltpu.VMEM((S, PS), F32),
            sem((NX - 1,)), sem((NX - 1,)),
            sem((NY - 1,)), sem((NY - 1,)),
            sem((NZ,)), sem((NZ,)),
            sem((2, NZ // 2)), sem((2, NZ // 2)),
            sem((2, NZ)), sem((2, NZ)),
            sem((NY - 1,)), sem((NY - 1,)),
            sem((NZ - 1,)), sem((NZ - 1,)),
            sem((NY - 1,)), sem((NY - 1,)),
            sem((NX - 1,)), sem((NX - 1,)),
            sem, sem,
            sem((NX - 1,)), sem((NX - 1,)),
            sem((NY - 1,)), sem((NY - 1,)),
            sem((NZ - 1,)), sem((NZ - 1,)),
            sem((2,)), sem((2,)),
        ],
        compiler_params=pltpu.CompilerParams(
            collective_id=0, has_side_effects=True, vmem_limit_bytes=48 * 1024 * 1024
        ),
    )(
        sp.reshape(M, PS), ss.reshape(M, S), mis.reshape(1, M), dep.reshape(1, M), cc,
        side.reshape(1, M), tr.reshape(S, S), cs.reshape(S, PS), nr.reshape(S, S),
        cm.reshape(1, S),
    )
    gram, grad, hess, cross, ngrad, coup = outs
    return (
        gram, grad.reshape(PS), hess.reshape(1, 1, S, S), cross.reshape(1, 1, S, PS),
        ngrad.reshape(1, 1, S), coup.reshape(1, 1, S, S),
    )


def solution(mesh):
    wide = P("sat", "seg", None, None)
    line = P("sat", "seg", None)
    return jax.shard_map(
        shards,
        mesh=mesh,
        in_specs=(wide, wide, line, line, P("sat", "seg"), line, wide, wide, wide, line),
        out_specs=(P("sat", None), P(), wide, wide, line, wide),
        check_vma=False,
    )
```

time: 481 us -> 84.9 us (0.18)
  the two profiles are of different devices: /device:TPU:16 before, /device:TPU:4 now
where the time goes in v1:
time: 84.9 us; the launch traced here: 84.6 us
  Pallas kernels  74.7 us (88%)
  local copies, waits for them, and re-layouts  8.53 us (10%)
  between operations  1.39 us (2%)
    pallas_call x1, Pallas kernels, shards(): pl.pallas_call(kernel, out_shape=[jax.ShapeDtypeStruct(s, F32) for s in s...  74.7 us
    unnamed x23, local copies, waits for them, and re-layouts  8.53 us

profile of v1, /device:TPU:4, one launch (start us, length us, event | category | flops | bytes accessed | tf_op | source)
XLA Modules:
  0.0 84.6 jit_solution(10830096236799162582)
XLA Ops:
  0.6 0.0 copy-start.1
  1.3 0.0 copy-start.3
  1.3 0.0 copy-start.7
  1.3 0.9 %copy.16 = bf16[1,1,320,64]{3,2,1,0:T(8,128)(2,1)S(1)} copy(bf16[1,1,320,64]{2,3,1,0:T(8,128)(2,1)} %param.11) | data formatting | bytes 81920 | tf_op args[1]
  2.3 0.0 copy-start.4
  2.3 0.0 copy-done.1
  2.3 0.0 copy-done.3
  2.3 0.0 copy-done.7
  2.3 0.6 copy-done.4
  3.0 0.0 copy-start
  3.0 1.1 %copy-done = bf16[1,1,320,1024]{3,2,1,0:T(8,128)(2,1)S(1)} copy-done((bf16[1,1,320,1024]{3,2,1,0:T(8,128)(2,1)S(1)}, bf16[1,1,320,1024]{3,2,1,0:T(8,128)(2,1)}, u32[]{:S(2)}) %copy-start) | copy-done | bytes 655384
  4.0 0.0 copy-start.2
  4.0 0.8 copy-done.2
  4.8 0.0 copy-start.5
  4.8 0.7 copy-done.5
  5.5 0.0 copy-start.6
  5.5 0.7 copy-done.6
  6.2 74.7 %shard_map.145 = (f32[64,1024]{1,0:T(8,128)S(1)}, f32[1,1024]{1,0:T(1,128)S(1)}, f32[64,64]{1,0:T(8,128)S(1)}, f32[64,1024]{1,0:T(8,128)S(1)}, f32[1,64]{1,0:T(1,128)S(1)}, /*index=5*/f32[64,64]{1,0:T(8,128)S(1)}) custom-call(bf16[320,1024]{1,0:T(8,128)(2,1)S(1)} %bitcast.14, bf16[320,64]{1,0:T(8,128)(2,1)S(1)} %bitcast.15, f32[1,320]{1,0:T(1,128)S(1)} %bitcast.23, ...), custom_call_target="tpu_custom_call" | custom-call | tf_op jit(solution)/shard_map/pallas_call | solution.py:366
  80.8 0.7 copy.24
  81.5 0.6 copy.25
  82.1 0.6 copy.26
  82.7 0.7 copy.27
  83.4 0.5 copy.28
  84.0 0.6 copy.29
Async XLA Ops:
  0.6 1.7 %copy-start.1 = (bf16[1,1,64,1024]{3,2,1,0:T(8,128)(2,1)S(1)}, bf16[1,1,64,1024]{3,2,1,0:T(8,128)(2,1)}, u32[]{:S(2)}) copy-start(bf16[1,1,64,1024]{3,2,1,0:T(8,128)(2,1)} %param.17) | copy-start | bytes 393220
  1.3 1.0 %copy-start.3 = (bf16[1,1,64,64]{3,2,1,0:T(8,128)(2,1)S(1)}, bf16[1,1,64,64]{3,2,1,0:T(8,128)(2,1)}, u32[]{:S(2)}) copy-start(bf16[1,1,64,64]{3,2,1,0:T(8,128)(2,1)} %param.16) | copy-start | bytes 24580
  1.3 1.0 %copy-start.7 = (f32[1,1,64]{2,1,0:T(1,128)S(1)}, f32[1,1,64]{2,1,0:T(1,128)}, u32[]{:S(2)}) copy-start(f32[1,1,64]{2,1,0:T(1,128)} %param.19) | copy-start | bytes 772
  2.3 0.7 copy-start.4
  3.0 1.1 %copy-start = (bf16[1,1,320,1024]{3,2,1,0:T(8,128)(2,1)S(1)}, bf16[1,1,320,1024]{3,2,1,0:T(8,128)(2,1)}, u32[]{:S(2)}) copy-start(bf16[1,1,320,1024]{3,2,1,0:T(8,128)(2,1)} %param.10) | copy-start | bytes 1966084
  4.0 0.8 copy-start.2
  4.8 0.7 copy-start.5
  5.5 0.7 copy-start.6

commit v2 on v1

--- a/solution.py
+++ b/solution.py
@@ -12,6 +12,8 @@
 
 NX, NY, NZ = 4, 8, 8
 M, S, PS = 320, 64, 1024
+VMEM_ALL = 67043328
+OUTS = [(64, PS), (1, PS), (S, S), (S, PS), (1, S), (S, S)]
 COLS = PS // NX
 HALF = NZ // 2 * 64
 
@@ -22,13 +24,19 @@
     )
 
 
+def dot1(a, b):
+    return lax.dot_general(a, b, (((1,), (1,)), ((), ())), preferred_element_type=F32)
+
+
 def kernel(
-    sp, ss, mis, dep, cc, side, tr, cs, nr, cm,
-    gram, grad, hess, cross, ngrad, coup,
-    A, G2, R0, RX1, RX2, W, RY, V, RZ, FIN,
+    sp_h, ss_h, mis_h, dep_h, cc, side_h, tr_h, cs_h, nr_h, cm_h,
+    gram_h, grad_h, hess_h, cross_h, ngrad_h, coup_h,
+    gram, grad, hess, cross, ngrad, coup, out_s,
+    sp, ss, mis, dep, side, tr, cs, nr, cm, in_s,
+    A, G2, R0, RX1, RX2, W, R1, V, R2, FA, FB,
     TX, TY, GC, GX, GY, GZ, HB, HC, HBr, HCr,
     tx_s, tx_r, ty_s, ty_r, core_s, core_r, x1_s, x1_r, x2_s, x2_r,
-    y_s, y_r, z_s, z_r, ay_s, ay_r, ax_s, ax_r,
+    p_s, p_r, q_s, q_r, ay_s, ay_r, ax_s, ax_r,
     gc_s, gc_r, gx_s, gx_r, gy_s, gy_r, gz_s, gz_r, h_s, h_r,
 ):
     sat = lax.axis_index("sat")
@@ -56,6 +64,26 @@
             device_id=dev, device_id_type=MESH,
         )
 
+    loads = [
+        pltpu.make_async_copy(a, b, in_s.at[i])
+        for i, (a, b) in enumerate(
+            [
+                (dep_h, dep), (nr_h, nr), (cs_h, cs), (tr_h, tr), (cm_h, cm),
+                (mis_h, mis), (side_h, side), (ss_h, ss), (sp_h, sp),
+            ]
+        )
+    ]
+    for load in loads:
+        load.start()
+    results = [
+        pltpu.make_async_copy(a, b, out_s.at[i])
+        for i, (a, b) in enumerate(
+            [
+                (gram, gram_h), (grad, grad_h), (hess, hess_h),
+                (cross, cross_h), (ngrad, ngrad_h), (coup, coup_h),
+            ]
+        )
+    ]
     barrier = pltpu.get_barrier_semaphore()
     partners = [core_dev, after, before]
     partners += [x_dev(k) for k in range(1, NX)]
@@ -67,6 +95,7 @@
     rows = lax.broadcasted_iota(jnp.int32, (M, M), 0)
     lanes = lax.broadcasted_iota(jnp.int32, (M, M), 1)
     count = cc[...]
+    loads[0].wait()
     used = jnp.where(lax.broadcasted_iota(jnp.int32, (1, M), 1) < count, dep[...], 0.0)
     through = jnp.sum(used, axis=1, keepdims=True)
     TX[x] = jnp.broadcast_to(through, (1, 128))
@@ -82,6 +111,8 @@
     link = jnp.where(seg < NX * NY - 1, 1.0, 0.0).astype(F32)
     r64 = lax.broadcasted_iota(jnp.int32, (S, S), 0)
     l64 = lax.broadcasted_iota(jnp.int32, (S, S), 1)
+    for load in loads[1:]:
+        load.wait()
     root = (jnp.where(r64 == l64, 1.0, 0.0) + nr[...]) * link
     pm = jnp.dot(
         root, cs[...].astype(F32), precision=highest, preferred_element_type=F32
@@ -112,11 +143,11 @@
     small = dot0(both, both, highest)
     wide = dot0(both, pm.astype(F32), highest)
     coup[...] = -small[:S, S:]
+    results[5].start()
     cres = jnp.sum(root * cm[...], axis=1, keepdims=True).astype(BF16).astype(F32)
     cres_row = jnp.sum(jnp.where(r64 == l64, cres, 0.0), axis=0, keepdims=True)
     state_grad = jnp.sum(both * cres, axis=0, keepdims=True)
     side_f = side[...].astype(F32)
-    side_col = jnp.sum(jnp.where(rows == lanes, side_f, 0.0), axis=1, keepdims=True)
     live_col = jnp.where(
         lax.broadcasted_iota(jnp.int32, (M, 1), 0) < count, 1.0, 0.0
     ).astype(F32)
@@ -131,35 +162,8 @@
     weight = jnp.sqrt(live_col / (1.0 + age * (4.0 / (M * NX * NY))))
     weight_row = jnp.sum(jnp.where(rows == lanes, weight, 0.0), axis=0, keepdims=True)
     A[:M, :] = (weight * sp[...].astype(F32)).astype(BF16)
-    state_rows = weight * ss[...].astype(F32)
-    pair = jnp.concatenate(
-        [state_rows * (1.0 - side_col), state_rows * side_col], axis=1
-    ).astype(BF16)
     res8 = jnp.broadcast_to(weight_row * mis[...], (8, M)).astype(BF16)
     cres8 = jnp.broadcast_to(cres_row, (8, S)).astype(BF16)
-    ws = A[:M, :]
-
-    pgram = dot0(pair, pair)
-    pcross = dot0(pair, ws)
-    pgrad = jnp.dot(res8, pair, preferred_element_type=F32)[0:1]
-    HC[...] = pcross[S:] - wide[S:]
-    HB[...] = jnp.zeros_like(HB)
-    HB[0:S, 0:S] = pgram[S:, S:] + small[S:, S:]
-    HB[S : S + 1, 0:S] = pgrad[:, S:] + state_grad[:, S:]
-
-    halo = [
-        copy(HC, HCr, h_s.at[0], h_r.at[0], after),
-        copy(HB, HBr, h_s.at[1], h_r.at[1], after),
-    ]
-
-    @pl.when(seg < NX * NY - 1)
-    def _():
-        for h in halo:
-            h.start()
-
-    cross[...] = pcross[:S] + wide[:S]
-    hess[...] = pgram[:S, :S] + small[:S, :S]
-    ngrad[...] = pgrad[:, :S] - state_grad[:, :S]
 
     def core_copy(zi):
         part = pl.ds(pl.multiple_of(zi * 64, 64), 64)
@@ -180,7 +184,7 @@
     lax.fori_loop(0, NZ, gram_step, 0)
 
     GC[0] = (
-        jnp.dot(res8, ws, preferred_element_type=F32)
+        jnp.dot(res8, A[:M, :], preferred_element_type=F32)
         - jnp.dot(cres8, pm, preferred_element_type=F32)
     )[0:1]
     gc = copy(GC.at[0], GC.at[1], gc_s, gc_r, core_dev)
@@ -225,6 +229,21 @@
     for k in range(1, NX):
         gx(k).start()
 
+    state_rows = weight_row * ss[...].astype(F32)
+    pair = jnp.concatenate(
+        [state_rows * (1.0 - side_f), state_rows * side_f], axis=0
+    ).astype(BF16)
+    pgram = dot1(pair, pair)
+    pcross = jnp.dot(pair, A[:M, :], preferred_element_type=F32)
+    pgrad = dot1(res8, pair)[0:1]
+    HC[...] = pcross[S:] - wide[S:]
+    HB[...] = jnp.zeros_like(HB)
+    HB[0:S, 0:S] = pgram[S:, S:] + small[S:, S:]
+    HB[S : S + 1, 0:S] = pgrad[:, S:] + state_grad[:, S:]
+    cross[...] = pcross[:S] + wide[:S]
+    hess[...] = pgram[:S, :S] + small[:S, :S]
+    ngrad[...] = pgrad[:, :S] - state_grad[:, :S]
+
     def x_second(j, _):
         for d in range(2):
             zi = d * (NZ // 2) + j
@@ -236,6 +255,16 @@
 
     lax.fori_loop(0, NZ // 2, x_second, 0)
 
+    halo = [
+        copy(HC, HCr, h_s.at[0], h_r.at[0], after),
+        copy(HB, HBr, h_s.at[1], h_r.at[1], after),
+    ]
+
+    @pl.when(seg < NX * NY - 1)
+    def _():
+        for h in halo:
+            h.start()
+
     for k in range(1, NX):
         gx(k).wait_recv()
     GY[y] = (GX[0] + GX[1]) + (GX[2] + GX[3])
@@ -251,16 +280,26 @@
         for d in range(2):
             x2(d, zi).wait_recv()
         own = R0[x, rows64(zi), :] + RX2[0, rows64(zi), :] + RX2[1, rows64(zi), :]
-        W[:, zi] = own.reshape(NY, 8, COLS)
+        own = own.reshape(NY, 8, COLS)
+        W[0, :, zi] = own[:, :, : COLS // 2]
+        W[1, zi] = own[:, :, COLS // 2 :]
         return 0
 
     lax.fori_loop(0, NZ, x_last, 0)
 
-    def yc(k):
-        return copy(W.at[(y + k) % NY], RY.at[k - 1], y_s.at[k - 1], y_r.at[k - 1], y_dev(k))
-
-    for k in range(1, NY):
-        yc(k).start()
+    lines = [(y, y_dev, z, z_dev), (z, z_dev, y, y_dev)]
+
+    def pc(g, k):
+        at, dev, _, _ = lines[g]
+        return copy(W.at[g, (at + k) % 8], R1.at[g, k - 1], p_s.at[g, k - 1], p_r.at[g, k - 1], dev(k))
+
+    def qc(g, k):
+        _, _, at, dev = lines[g]
+        return copy(V.at[g, (at + k) % 8], R2.at[g, k - 1], q_s.at[g, k - 1], q_r.at[g, k - 1], dev(k))
+
+    for k in range(1, 8):
+        for g in range(2):
+            pc(g, k).start()
     for k in range(1, NY):
         gy(k).wait_recv()
     part = GY[0]
@@ -282,16 +321,17 @@
         hess[...] = hess[...] + HBr[0:S, 0:S]
         ngrad[...] = ngrad[...] + HBr[S : S + 1, 0:S]
 
-    V[...] = W[y]
-    for k in range(1, NY):
-        yc(k).wait_recv()
-        V[...] = V[...] + RY[k - 1]
-
-    def zc(k):
-        return copy(V.at[(z + k) % NZ], RZ.at[k - 1], z_s.at[k - 1], z_r.at[k - 1], z_dev(k))
-
-    for k in range(1, NZ):
-        zc(k).start()
+    for i in (2, 3, 4):
+        results[i].start()
+
+    for g in range(2):
+        acc = W[g, lines[g][0]]
+        for k in range(1, 8):
+            pc(g, k).wait_recv()
+            acc = acc + R1[g, k - 1]
+        V[g] = acc
+        for k in range(1, 8):
+            qc(g, k).start()
     for k in range(1, NZ):
         gz(k).wait_recv()
     part = GZ[0]
@@ -299,43 +339,64 @@
         part = part + GZ[k]
     scale = 1.0 / (2 * NX * NY * NZ)
     grad[...] = part * scale
-
-    own = V[z]
-    for k in range(1, NZ):
-        zc(k).wait_recv()
-        own = own + RZ[k - 1]
-    FIN[x, y] = own * scale
-
-    def ay(k):
-        return copy(FIN.at[x, y], FIN.at[x, y], ay_s.at[k - 1], ay_r.at[k - 1], y_dev(k))
-
-    for k in range(1, NY):
-        ay(k).start()
-    for k in range(1, NY):
-        ay(k).wait_recv()
-
-    def ax(k):
-        return copy(FIN.at[x], FIN.at[x], ax_s.at[k - 1], ax_r.at[k - 1], x_dev(k))
-
-    for k in range(1, NX):
-        ax(k).start()
-    for k in range(1, NX):
-        ax(k).wait_recv()
+    results[1].start()
+
+    done = []
+    for g in range(2):
+        own = V[g, lines[g][2]]
+        for k in range(1, 8):
+            qc(g, k).wait_recv()
+            own = own + R2[g, k - 1]
+        done.append(own * scale)
+    FA[x, y] = done[0]
+    FB[y, x] = done[1]
+
+    def ay(g, k):
+        block = FA.at[x, y] if g == 0 else FB.at[y]
+        return copy(block, block, ay_s.at[g, k - 1], ay_r.at[g, k - 1], y_dev(k))
+
+    def ax(g, k):
+        block = FA.at[x] if g == 0 else FB.at[y, x]
+        return copy(block, block, ax_s.at[g, k - 1], ax_r.at[g, k - 1], x_dev(k))
+
+    for k in range(1, NY):
+        ay(0, k).start()
+    for k in range(1, NX):
+        ax(1, k).start()
+    for k in range(1, NX):
+        ax(1, k).wait_recv()
+    for k in range(1, NY):
+        ay(1, k).start()
+    for k in range(1, NY):
+        ay(0, k).wait_recv()
+    for k in range(1, NX):
+        ax(0, k).start()
+    for k in range(1, NY):
+        ay(1, k).wait_recv()
     for q in range(NX):
-        gram[:, q * COLS : (q + 1) * COLS] = FIN[q].reshape(64, COLS)
+        at = q * COLS + COLS // 2
+        gram[:, at : at + COLS // 2] = FB[:, q].reshape(64, COLS // 2)
+    for k in range(1, NX):
+        ax(0, k).wait_recv()
+    for q in range(NX):
+        gram[:, q * COLS : q * COLS + COLS // 2] = FA[q].reshape(64, COLS // 2)
+
+    results[0].start()
 
     for k in range(1, NX):
         tx(k).wait_send()
         gx(k).wait_send()
-        ax(k).wait_send()
+        for g in range(2):
+            ax(g, k).wait_send()
     for k in range(1, NY):
         ty(k).wait_send()
         gy(k).wait_send()
-        yc(k).wait_send()
-        ay(k).wait_send()
+        for g in range(2):
+            ay(g, k).wait_send()
+            pc(g, k).wait_send()
+            qc(g, k).wait_send()
     for k in range(1, NZ):
         gz(k).wait_send()
-        zc(k).wait_send()
     gc.wait_send()
 
     def drain(zi, _):
@@ -358,27 +419,56 @@
         for h in halo:
             h.wait_send()
 
+    for out in results:
+        out.wait()
+
+
+def put_out(*refs):
+    ins, outs, held, sems = refs[:6], refs[6:12], refs[12:18], refs[18]
+    into = [pltpu.make_async_copy(ins[i], held[i], sems.at[0, i]) for i in range(6)]
+    back = [pltpu.make_async_copy(held[i], outs[i], sems.at[1, i]) for i in range(6)]
+    for one in into:
+        one.start()
+    for one, two in zip(into, back):
+        one.wait()
+        two.start()
+    for two in back:
+        two.wait()
+
 
 def shards(sp, ss, mis, dep, cc, side, tr, cs, nr, cm):
     vmem = pl.BlockSpec(memory_space=pltpu.VMEM)
+    hbm = pl.BlockSpec(memory_space=pltpu.HBM)
     sem = pltpu.SemaphoreType.DMA
-    shapes = [(64, PS), (1, PS), (S, S), (S, PS), (1, S), (S, S)]
     outs = pl.pallas_call(
         kernel,
-        out_shape=[jax.ShapeDtypeStruct(s, F32) for s in shapes],
-        in_specs=[vmem] * 10,
-        out_specs=[vmem] * 6,
-        scratch_shapes=[
+        out_shape=[jax.ShapeDtypeStruct(s, F32) for s in OUTS],
+        in_specs=[vmem if i == 4 else hbm for i in range(10)],
+        out_specs=[hbm] * 6,
+        scratch_shapes=[pltpu.VMEM(s, F32) for s in OUTS]
+        + [
+            sem((6,)),
+            pltpu.VMEM((M, PS), BF16),
+            pltpu.VMEM((S, M), BF16),
+            pltpu.VMEM((1, M), F32),
+            pltpu.VMEM((1, M), F32),
+            pltpu.VMEM((1, M), jnp.int32),
+            pltpu.VMEM((S, S), BF16),
+            pltpu.VMEM((S, PS), BF16),
+            pltpu.VMEM((S, S), F32),
+            pltpu.VMEM((1, S), F32),
+            sem((9,)),
             pltpu.VMEM((M + S, PS), BF16),
             pltpu.VMEM((2, NX, 512, COLS), F32),
             pltpu.VMEM((NX, 512, COLS), F32),
             pltpu.VMEM((2, HALF, COLS), F32),
             pltpu.VMEM((2, 512, COLS), F32),
-            pltpu.VMEM((NY, NZ, 8, COLS), F32),
-            pltpu.VMEM((NY - 1, NZ, 8, COLS), F32),
-            pltpu.VMEM((NZ, 8, COLS), F32),
-            pltpu.VMEM((NZ - 1, 8, COLS), F32),
-            pltpu.VMEM((NX, NY, 8, COLS), F32),
+            pltpu.VMEM((2, 8, 8, 8, COLS // 2), F32),
+            pltpu.VMEM((2, 7, 8, 8, COLS // 2), F32),
+            pltpu.VMEM((2, 8, 8, COLS // 2), F32),
+            pltpu.VMEM((2, 7, 8, COLS // 2), F32),
+            pltpu.VMEM((NX, NY, 8, COLS // 2), F32),
+            pltpu.VMEM((NY, NX, 8, COLS // 2), F32),
             pltpu.VMEM((NX, 1, 128), F32),
             pltpu.VMEM((NY, 1, 128), F32),
             pltpu.VMEM((2, 1, PS), F32),
@@ -394,10 +484,10 @@
             sem((NZ,)), sem((NZ,)),
             sem((2, NZ // 2)), sem((2, NZ // 2)),
             sem((2, NZ)), sem((2, NZ)),
-            sem((NY - 1,)), sem((NY - 1,)),
-            sem((NZ - 1,)), sem((NZ - 1,)),
-            sem((NY - 1,)), sem((NY - 1,)),
-            sem((NX - 1,)), sem((NX - 1,)),
+            sem((2, 7)), sem((2, 7)),
+            sem((2, 7)), sem((2, 7)),
+            sem((2, NY - 1)), sem((2, NY - 1)),
+            sem((2, NX - 1)), sem((2, NX - 1)),
             sem, sem,
             sem((NX - 1,)), sem((NX - 1,)),
             sem((NY - 1,)), sem((NY - 1,)),
@@ -405,13 +495,21 @@
             sem((2,)), sem((2,)),
         ],
         compiler_params=pltpu.CompilerParams(
-            collective_id=0, has_side_effects=True, vmem_limit_bytes=48 * 1024 * 1024
+            collective_id=0, has_side_effects=True, vmem_limit_bytes=VMEM_ALL
         ),
     )(
-        sp.reshape(M, PS), ss.reshape(M, S), mis.reshape(1, M), dep.reshape(1, M), cc,
+        sp.reshape(M, PS), ss.reshape(M, S).T, mis.reshape(1, M), dep.reshape(1, M), cc,
         side.reshape(1, M), tr.reshape(S, S), cs.reshape(S, PS), nr.reshape(S, S),
         cm.reshape(1, S),
     )
+    outs = pl.pallas_call(
+        put_out,
+        out_shape=[jax.ShapeDtypeStruct(s, F32) for s in OUTS],
+        in_specs=[hbm] * 6,
+        out_specs=[hbm] * 6,
+        scratch_shapes=[pltpu.VMEM(s, F32) for s in OUTS] + [sem((2, 6))],
+        compiler_params=pltpu.CompilerParams(vmem_limit_bytes=VMEM_ALL),
+    )(*outs)
     gram, grad, hess, cross, ngrad, coup = outs
     return (
         gram, grad.reshape(PS), hess.reshape(1, 1, S, S), cross.reshape(1, 1, S, PS),

time: 84.9 us -> 75 us (0.88)
  the two profiles are of different devices: /device:TPU:4 before, /device:TPU:64 now
where the time goes in v2:
time: 75 us; the launch traced here: 74.8 us
  Pallas kernels  73.5 us (98%)
  between operations  1.29 us (2%)
    pallas_call x1, Pallas kernels, shards(): pl.pallas_call(kernel, out_shape=[jax.ShapeDtypeStruct(s, F32) for s in O...  71.7 us
    pallas_call x1, Pallas kernels, shards(): pl.pallas_call(put_out, out_shape=[jax.ShapeDtypeStruct(s, F32) for s in...  1.87 us

profile of v2, /device:TPU:64, one launch (start us, length us, event | category | flops | bytes accessed | tf_op | source)
XLA Modules:
  0.0 74.8 jit_solution(2594023125080858770)
XLA Ops:
  1.3 71.7 %shard_map.145 = (f32[64,1024]{1,0:T(8,128)}, f32[1,1024]{1,0:T(1,128)}, f32[64,64]{1,0:T(8,128)}, f32[64,1024]{1,0:T(8,128)}, f32[1,64]{1,0:T(1,128)}, /*index=5*/f32[64,64]{1,0:T(8,128)}) custom-call(bf16[320,1024]{1,0:T(8,128)(2,1)} %bitcast.16, bf16[64,320]{1,0:T(8,128)(2,1)} %bitcast.18, f32[1,320]{1,0:T(1,128)} %bitcast.21, f32[1,320]{1,0:T(1,128)} %bitcast.22, ...), custom_call_target="tpu_custom_call" | custom-call | tf_op jit(solution)/shard_map/pallas_call | solution.py:443
  73.0 1.9 %shard_map.146 = (f32[64,1024]{1,0:T(8,128)}, f32[1,1024]{1,0:T(1,128)}, f32[64,64]{1,0:T(8,128)}, f32[64,1024]{1,0:T(8,128)}, f32[1,64]{1,0:T(1,128)}, /*index=5*/f32[64,64]{1,0:T(8,128)}) custom-call(f32[64,1024]{1,0:T(8,128)} %get-tuple-element.18.refs_0_, f32[1,1024]{1,0:T(1,128)} %get-tuple-element.19.refs_1_, f32[64,64]{1,0:T(8,128)} %get-tuple-element.20.refs_2_, ...), custom_call_target="tpu_custom_call" | custom-call | tf_op jit(solution)/shard_map/pallas_call | solution.py:505

commit v3 on v2

--- a/solution.py
+++ b/solution.py
@@ -14,8 +14,6 @@
 M, S, PS = 320, 64, 1024
 VMEM_ALL = 67043328
 OUTS = [(64, PS), (1, PS), (S, S), (S, PS), (1, S), (S, S)]
-COLS = PS // NX
-HALF = NZ // 2 * 64
 
 
 def dot0(a, b, precision=None):
@@ -33,10 +31,10 @@
     gram_h, grad_h, hess_h, cross_h, ngrad_h, coup_h,
     gram, grad, hess, cross, ngrad, coup, out_s,
     sp, ss, mis, dep, side, tr, cs, nr, cm, in_s,
-    A, G2, R0, RX1, RX2, W, R1, V, R2, FA, FB,
+    A, G2, R0, RX1, RX2, W, R1, V, R2, FA, FB, FAr, FBr,
     TX, TY, GC, GX, GY, GZ, HB, HC, HBr, HCr,
     tx_s, tx_r, ty_s, ty_r, core_s, core_r, x1_s, x1_r, x2_s, x2_r,
-    p_s, p_r, q_s, q_r, ay_s, ay_r, ax_s, ax_r,
+    p_s, p_r, q_s, q_r, fin_s, fin_r, ay_s, ay_r, ax_s, ax_r,
     gc_s, gc_r, gx_s, gx_r, gy_s, gy_r, gz_s, gz_r, h_s, h_r,
 ):
     sat = lax.axis_index("sat")
@@ -117,7 +115,7 @@
     pm = jnp.dot(
         root, cs[...].astype(F32), precision=highest, preferred_element_type=F32
     ).astype(BF16)
-    A[M:, :] = pm
+    A[M:, :PS] = pm
     inner = jnp.sum(jnp.where(lanes < rows, used, 0.0), axis=1, keepdims=True)
 
     for k in range(1, NX):
@@ -161,64 +159,109 @@
     age = inner + prior[:, 0:1]
     weight = jnp.sqrt(live_col / (1.0 + age * (4.0 / (M * NX * NY))))
     weight_row = jnp.sum(jnp.where(rows == lanes, weight, 0.0), axis=0, keepdims=True)
-    A[:M, :] = (weight * sp[...].astype(F32)).astype(BF16)
+    A[:M, :PS] = (weight * sp[...].astype(F32)).astype(BF16)
+    A[:, PS:] = A[:, : PS // 2]
     res8 = jnp.broadcast_to(weight_row * mis[...], (8, M)).astype(BF16)
     cres8 = jnp.broadcast_to(cres_row, (8, S)).astype(BF16)
 
-    def core_copy(zi):
-        part = pl.ds(pl.multiple_of(zi * 64, 64), 64)
+    def slot(i, dd, half):
+        return (i + dd) % NX, 4 if dd == 2 else 2 * dd + half
+
+    def core_copy(i, dd, half):
+        q, n = slot(i, dd, half)
         return copy(
-            G2.at[1 - c, :, part, :], R0.at[:, part, :], core_s.at[zi], core_r.at[zi], core_dev
+            G2.at[1 - c, q, n], R0.at[q, n],
+            core_s.at[dd, half * 4 + i], core_r.at[dd, half * 4 + i], core_dev,
         )
 
-    def gram_step(i, _):
-        zi = (i % 2) * (NZ // 2) + i // 2
-        g = dot0(A[:, pl.ds(pl.multiple_of(zi * 128, 128), 128)], A[...])
-        part = pl.ds(pl.multiple_of(zi * 64, 64), 64)
-        for q in range(NX):
-            G2[0, q, part, :] = g[:64, q * COLS : (q + 1) * COLS]
-            G2[1, q, part, :] = g[64:, q * COLS : (q + 1) * COLS]
-        core_copy(zi).start()
-        return 0
-
-    lax.fori_loop(0, NZ, gram_step, 0)
+    def gram_half(half):
+        def step(i, _):
+            at = pl.multiple_of((half * 4 + i) * 128, 128)
+            g = dot0(A[:, pl.ds(at, 128)], A[:, pl.ds(at, 640)])
+            for d in range(5 - half):
+                q, n = slot(i, d // 2, half)
+                G2[d % 2, q, n] = g[:, d * 128 : (d + 1) * 128]
+            for dd in range(2):
+                core_copy(i, dd, half).start()
+            if half == 0:
+
+                @pl.when(c == 1)
+                def _():
+                    core_copy(i, 2, 0).start()
+
+            return 0
+
+        lax.fori_loop(0, 4, step, 0)
+
+    far, right, left = (x + 2) % NX, (x + 1) % NX, (x + 3) % NX
+
+    def x1(n):
+        d = 1 if n == 4 else n % 2
+        return copy(R0.at[far, n], RX1.at[n], x1_s.at[n], x1_r.at[n], x_dev(1 if d == 0 else 3))
+
+    def x2(d, n):
+        return copy(
+            R0.at[right if d == 0 else left, n], RX2.at[d, n],
+            x2_s.at[d, n], x2_r.at[d, n], x_dev(1 if d == 0 else 3),
+        )
+
+    def x_first(n):
+        d = 1 if n == 4 else n % 2
+        for i in range(4):
+            core_copy(i, n // 2, 0 if n == 4 else n % 2).wait_recv()
+        R0[:, n] = R0[:, n] + G2[c, :, n]
+        x1(n).start()
+        x2(1 - d, n).start()
+
+    def x_second(n):
+        d = 1 if n == 4 else n % 2
+        dest = right if d == 0 else left
+        x1(n).wait_recv()
+        R0[dest, n] = R0[dest, n] + RX1[n]
+        x2(d, n).start()
+
+    def spread(block, strip):
+        parts = block.reshape(NY, 2, 8, 128)
+        W[0, :, strip] = parts[:, 0]
+        W[1, strip] = parts[:, 1]
+
+    def x_last(n):
+        for d in range(2):
+            x2(d, n).wait_recv()
+        own = R0[x, n] + RX2[0, n] + RX2[1, n]
+        dd = n // 2
+        i = (x + 4 - dd) % NX + (0 if n == 4 else (n % 2) * 4)
+        j = (i + 2 * dd + c) % NZ
+        if dd == 0:
+            spread(own, i)
+
+            @pl.when(c == 1)
+            def _():
+                spread(own.T, j)
+
+        else:
+            spread(own, i)
+            spread(own.T, j)
+
+    def only_core0(step, n):
+        @pl.when(c == 0)
+        def _():
+            step(n)
+
+    gram_half(0)
+    x_first(0)
+    x_first(2)
+    gram_half(1)
+    only_core0(x_first, 4)
+    x_first(1)
+    x_first(3)
 
     GC[0] = (
-        jnp.dot(res8, A[:M, :], preferred_element_type=F32)
+        jnp.dot(res8, A[:M, :PS], preferred_element_type=F32)
         - jnp.dot(cres8, pm, preferred_element_type=F32)
     )[0:1]
     gc = copy(GC.at[0], GC.at[1], gc_s, gc_r, core_dev)
     gc.start()
-
-    far, right, left = (x + 2) % NX, (x + 1) % NX, (x + 3) % NX
-
-    def rows64(j):
-        return pl.ds(pl.multiple_of(j * 64, 64), 64)
-
-    def x1(d, j):
-        zi = d * (NZ // 2) + j
-        return copy(
-            R0.at[far, rows64(zi), :], RX1.at[d, rows64(j), :],
-            x1_s.at[d, j], x1_r.at[d, j], x_dev(1 if d == 0 else 3),
-        )
-
-    def x2(d, zi):
-        return copy(
-            R0.at[right if d == 0 else left, rows64(zi), :], RX2.at[d, rows64(zi), :],
-            x2_s.at[d, zi], x2_r.at[d, zi], x_dev(1 if d == 0 else 3),
-        )
-
-    def x_first(j, _):
-        for d in range(2):
-            zi = d * (NZ // 2) + j
-            core_copy(zi).wait_recv()
-            R0[:, rows64(zi), :] = R0[:, rows64(zi), :] + G2[c, :, rows64(zi), :]
-            x1(d, j).start()
-        for d in range(2):
-            x2(1 - d, d * (NZ // 2) + j).start()
-        return 0
-
-    lax.fori_loop(0, NZ // 2, x_first, 0)
 
     gc.wait_recv()
     GX[x] = GC[0] + GC[1]
@@ -234,7 +277,7 @@
         [state_rows * (1.0 - side_f), state_rows * side_f], axis=0
     ).astype(BF16)
     pgram = dot1(pair, pair)
-    pcross = jnp.dot(pair, A[:M, :], preferred_element_type=F32)
+    pcross = jnp.dot(pair, A[:M, :PS], preferred_element_type=F32)
     pgrad = dot1(res8, pair)[0:1]
     HC[...] = pcross[S:] - wide[S:]
     HB[...] = jnp.zeros_like(HB)
@@ -244,16 +287,11 @@
     hess[...] = pgram[:S, :S] + small[:S, :S]
     ngrad[...] = pgrad[:, :S] - state_grad[:, :S]
 
-    def x_second(j, _):
-        for d in range(2):
-            zi = d * (NZ // 2) + j
-            dest = right if d == 0 else left
-            x1(d, j).wait_recv()
-            R0[dest, rows64(zi), :] = R0[dest, rows64(zi), :] + RX1[d, rows64(j), :]
-            x2(d, zi).start()
-        return 0
-
-    lax.fori_loop(0, NZ // 2, x_second, 0)
+    x_second(0)
+    x_second(2)
+    only_core0(x_second, 4)
+    x_second(1)
+    x_second(3)
 
     halo = [
         copy(HC, HCr, h_s.at[0], h_r.at[0], after),
@@ -275,17 +313,11 @@
     for k in range(1, NY):
         gy(k).start()
 
-    def x_last(i, _):
-        zi = (i % 2) * (NZ // 2) + i // 2
-        for d in range(2):
-            x2(d, zi).wait_recv()
-        own = R0[x, rows64(zi), :] + RX2[0, rows64(zi), :] + RX2[1, rows64(zi), :]
-        own = own.reshape(NY, 8, COLS)
-        W[0, :, zi] = own[:, :, : COLS // 2]
-        W[1, zi] = own[:, :, COLS // 2 :]
-        return 0
-
-    lax.fori_loop(0, NZ, x_last, 0)
+    x_last(0)
+    x_last(2)
+    only_core0(x_last, 4)
+    x_last(1)
+    x_last(3)
 
     lines = [(y, y_dev, z, z_dev), (z, z_dev, y, y_dev)]
 
@@ -373,14 +405,27 @@
         ax(0, k).start()
     for k in range(1, NY):
         ay(1, k).wait_recv()
+    for k in range(1, NX):
+        ax(0, k).wait_recv()
+
+    mine, theirs = pl.ds(4 * c, 4), pl.ds(4 * (1 - c), 4)
+    swap = [
+        copy(FA.at[:, theirs], FAr, fin_s.at[0], fin_r.at[0], core_dev),
+        copy(FB.at[theirs], FBr, fin_s.at[1], fin_r.at[1], core_dev),
+    ]
+    for one in swap:
+        one.start()
+
+    def place(owner, first, second):
+        at = pl.multiple_of(((owner + NZ - z) % NZ) * 128, 128)
+        gram[:, pl.ds(at, 128)] = jnp.stack([first, second], axis=1).reshape(64, 128)
+
     for q in range(NX):
-        at = q * COLS + COLS // 2
-        gram[:, at : at + COLS // 2] = FB[:, q].reshape(64, COLS // 2)
-    for k in range(1, NX):
-        ax(0, k).wait_recv()
+        place(2 * q + c, FA[q, mine], FB[mine, q])
+    for one in swap:
+        one.wait_recv()
     for q in range(NX):
-        gram[:, q * COLS : q * COLS + COLS // 2] = FA[q].reshape(64, COLS // 2)
-
+        place(2 * q + 1 - c, FAr[q], FBr[:, q])
     results[0].start()
 
     for k in range(1, NX):
@@ -399,20 +444,26 @@
         gz(k).wait_send()
     gc.wait_send()
 
-    def drain(zi, _):
-        core_copy(zi).wait_send()
+    for one in swap:
+        one.wait_send()
+    for half in range(2):
+        for i in range(4):
+            for dd in range(2):
+                core_copy(i, dd, half).wait_send()
+
+    def x_drain(n):
+        x1(n).wait_send()
         for d in range(2):
-            x2(d, zi).wait_send()
-        return 0
-
-    lax.fori_loop(0, NZ, drain, 0)
-
-    def drain1(j, _):
-        for d in range(2):
-            x1(d, j).wait_send()
-        return 0
-
-    lax.fori_loop(0, NZ // 2, drain1, 0)
+            x2(d, n).wait_send()
+
+    for n in range(4):
+        x_drain(n)
+    only_core0(x_drain, 4)
+
+    @pl.when(c == 1)
+    def _():
+        for i in range(4):
+            core_copy(i, 2, 0).wait_send()
 
     @pl.when(seg < NX * NY - 1)
     def _():
@@ -458,17 +509,19 @@
             pltpu.VMEM((S, S), F32),
             pltpu.VMEM((1, S), F32),
             sem((9,)),
-            pltpu.VMEM((M + S, PS), BF16),
-            pltpu.VMEM((2, NX, 512, COLS), F32),
-            pltpu.VMEM((NX, 512, COLS), F32),
-            pltpu.VMEM((2, HALF, COLS), F32),
-            pltpu.VMEM((2, 512, COLS), F32),
-            pltpu.VMEM((2, 8, 8, 8, COLS // 2), F32),
-            pltpu.VMEM((2, 7, 8, 8, COLS // 2), F32),
-            pltpu.VMEM((2, 8, 8, COLS // 2), F32),
-            pltpu.VMEM((2, 7, 8, COLS // 2), F32),
-            pltpu.VMEM((NX, NY, 8, COLS // 2), F32),
-            pltpu.VMEM((NY, NX, 8, COLS // 2), F32),
+            pltpu.VMEM((M + S, PS + PS // 2), BF16),
+            pltpu.VMEM((2, NX, 5, 128, 128), F32),
+            pltpu.VMEM((NX, 5, 128, 128), F32),
+            pltpu.VMEM((5, 128, 128), F32),
+            pltpu.VMEM((2, 5, 128, 128), F32),
+            pltpu.VMEM((2, 8, 8, 8, 128), F32),
+            pltpu.VMEM((2, 7, 8, 8, 128), F32),
+            pltpu.VMEM((2, 8, 8, 128), F32),
+            pltpu.VMEM((2, 7, 8, 128), F32),
+            pltpu.VMEM((NX, NY, 8, 128), F32),
+            pltpu.VMEM((NY, NX, 8, 128), F32),
+            pltpu.VMEM((NX, 4, 8, 128), F32),
+            pltpu.VMEM((4, NX, 8, 128), F32),
             pltpu.VMEM((NX, 1, 128), F32),
             pltpu.VMEM((NY, 1, 128), F32),
             pltpu.VMEM((2, 1, PS), F32),
@@ -481,11 +534,12 @@
             pltpu.VMEM((S, PS), F32),
             sem((NX - 1,)), sem((NX - 1,)),
             sem((NY - 1,)), sem((NY - 1,)),
-            sem((NZ,)), sem((NZ,)),
-            sem((2, NZ // 2)), sem((2, NZ // 2)),
-            sem((2, NZ)), sem((2, NZ)),
+            sem((3, 8)), sem((3, 8)),
+            sem((5,)), sem((5,)),
+            sem((2, 5)), sem((2, 5)),
             sem((2, 7)), sem((2, 7)),
             sem((2, 7)), sem((2, 7)),
+            sem((2,)), sem((2,)),
             sem((2, NY - 1)), sem((2, NY - 1)),
             sem((2, NX - 1)), sem((2, NX - 1)),
             sem, sem,

time: 75 us -> 71.8 us (0.957)
  the two profiles are of different devices: /device:TPU:64 before, /device:TPU:1 now
where the time goes in v3:
time: 71.8 us; the launch traced here: 71.7 us
  Pallas kernels  70.4 us (98%)
  between operations  1.29 us (2%)
    pallas_call x1, Pallas kernels, shards(): pl.pallas_call(kernel, out_shape=[jax.ShapeDtypeStruct(s, F32) for s in O...  68.5 us
    pallas_call x1, Pallas kernels, shards(): pl.pallas_call(put_out, out_shape=[jax.ShapeDtypeStruct(s, F32) for s in...  1.87 us

profile of v3, /device:TPU:1, one launch (start us, length us, event | category | flops | bytes accessed | tf_op | source)
XLA Modules:
  0.0 71.7 jit_solution(7410604557223202414)
XLA Ops:
  1.3 68.5 %shard_map.145 = (f32[64,1024]{1,0:T(8,128)}, f32[1,1024]{1,0:T(1,128)}, f32[64,64]{1,0:T(8,128)}, f32[64,1024]{1,0:T(8,128)}, f32[1,64]{1,0:T(1,128)}, /*index=5*/f32[64,64]{1,0:T(8,128)}) custom-call(bf16[320,1024]{1,0:T(8,128)(2,1)} %bitcast.16, bf16[64,320]{1,0:T(8,128)(2,1)} %bitcast.18, f32[1,320]{1,0:T(1,128)} %bitcast.21, f32[1,320]{1,0:T(1,128)} %bitcast.22, ...), custom_call_target="tpu_custom_call" | custom-call | tf_op jit(solution)/shard_map/pallas_call | solution.py:494
  69.8 1.9 %shard_map.146 = (f32[64,1024]{1,0:T(8,128)}, f32[1,1024]{1,0:T(1,128)}, f32[64,64]{1,0:T(8,128)}, f32[64,1024]{1,0:T(8,128)}, f32[1,64]{1,0:T(1,128)}, /*index=5*/f32[64,64]{1,0:T(8,128)}) custom-call(f32[64,1024]{1,0:T(8,128)} %get-tuple-element.18.refs_0_, f32[1,1024]{1,0:T(1,128)} %get-tuple-element.19.refs_1_, f32[64,64]{1,0:T(8,128)} %get-tuple-element.20.refs_2_, ...), custom_call_target="tpu_custom_call" | custom-call | tf_op jit(solution)/shard_map/pallas_call | solution.py:559

commit v4 on v3

--- a/solution.py
+++ b/solution.py
@@ -32,10 +32,10 @@
     gram, grad, hess, cross, ngrad, coup, out_s,
     sp, ss, mis, dep, side, tr, cs, nr, cm, in_s,
     A, G2, R0, RX1, RX2, W, R1, V, R2, FA, FB, FAr, FBr,
-    TX, TY, GC, GX, GY, GZ, HB, HC, HBr, HCr,
+    TX, TY, GC, GX, GY, GZ, HB, HC, HBr, HCr, HBq, HCq,
     tx_s, tx_r, ty_s, ty_r, core_s, core_r, x1_s, x1_r, x2_s, x2_r,
     p_s, p_r, q_s, q_r, fin_s, fin_r, ay_s, ay_r, ax_s, ax_r,
-    gc_s, gc_r, gx_s, gx_r, gy_s, gy_r, gz_s, gz_r, h_s, h_r,
+    gc_s, gc_r, gx_s, gx_r, gy_s, gy_r, gz_s, gz_r, h_s, h_r, q_h_s, q_h_r,
 ):
     sat = lax.axis_index("sat")
     seg = lax.axis_index("seg")
@@ -52,9 +52,6 @@
 
     def z_dev(k):
         return (((z + k) % NZ) * 2 + c, seg)
-
-    after = (sat, (seg + 1) % (NX * NY))
-    before = (sat, (seg + NX * NY - 1) % (NX * NY))
 
     def copy(src, dst, send, recv, dev):
         return pltpu.make_async_remote_copy(
@@ -83,7 +80,7 @@
         )
     ]
     barrier = pltpu.get_barrier_semaphore()
-    partners = [core_dev, after, before]
+    partners = [core_dev]
     partners += [x_dev(k) for k in range(1, NX)]
     partners += [y_dev(k) for k in range(1, NY)]
     partners += [z_dev(k) for k in range(1, NZ)]
@@ -287,18 +284,33 @@
     hess[...] = pgram[:S, :S] + small[:S, :S]
     ngrad[...] = pgrad[:, :S] - state_grad[:, :S]
 
+
+    pass_halo = [
+        copy(HC, HCq, q_h_s.at[0], q_h_r.at[0], y_dev(1)),
+        copy(HB, HBq, q_h_s.at[1], q_h_r.at[1], y_dev(1)),
+    ]
+    halo = [
+        copy(HC, HCr, h_s.at[0], h_r.at[0], x_dev(1)),
+        copy(HB, HBr, h_s.at[1], h_r.at[1], x_dev(1)),
+    ]
+    relay = [
+        copy(HCq, HCr, h_s.at[0], h_r.at[0], x_dev(1)),
+        copy(HBq, HBr, h_s.at[1], h_r.at[1], x_dev(1)),
+    ]
+    last_x = x == NX - 1
+
+    @pl.when(last_x & (y < NY - 1))
+    def _():
+        for h in pass_halo:
+            h.start()
+
     x_second(0)
     x_second(2)
     only_core0(x_second, 4)
     x_second(1)
     x_second(3)
 
-    halo = [
-        copy(HC, HCr, h_s.at[0], h_r.at[0], after),
-        copy(HB, HBr, h_s.at[1], h_r.at[1], after),
-    ]
-
-    @pl.when(seg < NX * NY - 1)
+    @pl.when(x < NX - 1)
     def _():
         for h in halo:
             h.start()
@@ -321,17 +333,45 @@
 
     lines = [(y, y_dev, z, z_dev), (z, z_dev, y, y_dev)]
 
-    def pc(g, k):
+    def pc(g, d, j):
         at, dev, _, _ = lines[g]
-        return copy(W.at[g, (at + k) % 8], R1.at[g, k - 1], p_s.at[g, k - 1], p_r.at[g, k - 1], dev(k))
+        to = 1 if d == 0 else -1
+        src = W.at[g, (at + to * (j + 1) + 8) % 8]
+        dst = R1.at[g, d, j - 1]
+        if j == 3:
+            src, dst = src.at[pl.ds(4 * d, 4)], dst.at[pl.ds(4 * d, 4)]
+        return copy(src, dst, p_s.at[g, d, j - 1], p_r.at[g, d, j - 1], dev((to * j) % 8))
+
+    def pn(g, d):
+        at, dev, _, _ = lines[g]
+        to = 1 if d == 0 else -1
+        return copy(
+            W.at[g, (at + to + 8) % 8], R1.at[g, d, 3], p_s.at[g, d, 3], p_r.at[g, d, 3],
+            dev(to % 8),
+        )
 
     def qc(g, k):
         _, _, at, dev = lines[g]
         return copy(V.at[g, (at + k) % 8], R2.at[g, k - 1], q_s.at[g, k - 1], q_r.at[g, k - 1], dev(k))
 
-    for k in range(1, 8):
+    for j in (3, 2, 1):
         for g in range(2):
-            pc(g, k).start()
+            for d in range(2):
+                pc(g, d, j).start()
+    for g in range(2):
+        for d in range(2):
+            for j in (1, 2, 3):
+                pc(g, d, j).wait_recv()
+            at = (lines[g][0] + (1 if d == 0 else 7)) % 8
+            lo, hi = 4 * d, 4 * (1 - d)
+            W[g, at, pl.ds(lo, 4)] = (
+                W[g, at, pl.ds(lo, 4)]
+                + R1[g, d, 0, pl.ds(lo, 4)] + R1[g, d, 1, pl.ds(lo, 4)] + R1[g, d, 2, pl.ds(lo, 4)]
+            )
+            W[g, at, pl.ds(hi, 4)] = (
+                W[g, at, pl.ds(hi, 4)] + R1[g, d, 0, pl.ds(hi, 4)] + R1[g, d, 1, pl.ds(hi, 4)]
+            )
+            pn(g, d).start()
     for k in range(1, NY):
         gy(k).wait_recv()
     part = GY[0]
@@ -345,23 +385,17 @@
     for k in range(1, NZ):
         gz(k).start()
 
-    @pl.when(seg > 0)
+    @pl.when(last_x & (y > 0))
     def _():
-        for h in halo:
+        for h, r in zip(pass_halo, relay):
             h.wait_recv()
-        cross[...] = cross[...] + HCr[...]
-        hess[...] = hess[...] + HBr[0:S, 0:S]
-        ngrad[...] = ngrad[...] + HBr[S : S + 1, 0:S]
-
-    for i in (2, 3, 4):
-        results[i].start()
+            r.start()
+
 
     for g in range(2):
-        acc = W[g, lines[g][0]]
-        for k in range(1, 8):
-            pc(g, k).wait_recv()
-            acc = acc + R1[g, k - 1]
-        V[g] = acc
+        for d in range(2):
+            pn(g, d).wait_recv()
+        V[g] = W[g, lines[g][0]] + R1[g, 0, 3] + R1[g, 1, 3]
         for k in range(1, 8):
             qc(g, k).start()
     for k in range(1, NZ):
@@ -399,6 +433,18 @@
         ax(1, k).wait_recv()
     for k in range(1, NY):
         ay(1, k).start()
+
+    @pl.when(seg > 0)
+    def _():
+        for h in halo:
+            h.wait_recv()
+        cross[...] = cross[...] + HCr[...]
+        hess[...] = hess[...] + HBr[0:S, 0:S]
+        ngrad[...] = ngrad[...] + HBr[S : S + 1, 0:S]
+
+    for i in (2, 3, 4):
+        results[i].start()
+
     for k in range(1, NY):
         ay(0, k).wait_recv()
     for k in range(1, NX):
@@ -438,7 +484,6 @@
         gy(k).wait_send()
         for g in range(2):
             ay(g, k).wait_send()
-            pc(g, k).wait_send()
             qc(g, k).wait_send()
     for k in range(1, NZ):
         gz(k).wait_send()
@@ -465,7 +510,18 @@
         for i in range(4):
             core_copy(i, 2, 0).wait_send()
 
-    @pl.when(seg < NX * NY - 1)
+    for g in range(2):
+        for d in range(2):
+            for j in (1, 2, 3):
+                pc(g, d, j).wait_send()
+            pn(g, d).wait_send()
+
+    @pl.when(last_x & (y < NY - 1))
+    def _():
+        for h in pass_halo:
+            h.wait_send()
+
+    @pl.when((x < NX - 1) | (y > 0))
     def _():
         for h in halo:
             h.wait_send()
@@ -515,7 +571,7 @@
             pltpu.VMEM((5, 128, 128), F32),
             pltpu.VMEM((2, 5, 128, 128), F32),
             pltpu.VMEM((2, 8, 8, 8, 128), F32),
-            pltpu.VMEM((2, 7, 8, 8, 128), F32),
+            pltpu.VMEM((2, 2, 4, 8, 8, 128), F32),
             pltpu.VMEM((2, 8, 8, 128), F32),
             pltpu.VMEM((2, 7, 8, 128), F32),
             pltpu.VMEM((NX, NY, 8, 128), F32),
@@ -532,12 +588,14 @@
             pltpu.VMEM((S, PS), F32),
             pltpu.VMEM((72, 128), F32),
             pltpu.VMEM((S, PS), F32),
+            pltpu.VMEM((72, 128), F32),
+            pltpu.VMEM((S, PS), F32),
             sem((NX - 1,)), sem((NX - 1,)),
             sem((NY - 1,)), sem((NY - 1,)),
             sem((3, 8)), sem((3, 8)),
             sem((5,)), sem((5,)),
             sem((2, 5)), sem((2, 5)),
-            sem((2, 7)), sem((2, 7)),
+            sem((2, 2, 4)), sem((2, 2, 4)),
             sem((2, 7)), sem((2, 7)),
             sem((2,)), sem((2,)),
             sem((2, NY - 1)), sem((2, NY - 1)),
@@ -546,6 +604,7 @@
             sem((NX - 1,)), sem((NX - 1,)),
             sem((NY - 1,)), sem((NY - 1,)),
             sem((NZ - 1,)), sem((NZ - 1,)),
+            sem((2,)), sem((2,)),
             sem((2,)), sem((2,)),
         ],
         compiler_params=pltpu.CompilerParams(

time: 71.8 us -> 68.6 us (0.955)
  Pallas kernels: 70.4 us -> 67.2 us
    pallas_call x1, Pallas kernels: 68.5 us -> 65.3 us  [shards(): pl.pallas_call(kernel, out_shape=[jax.ShapeDtypeStruct(s, F32) for s in O...]
where the time goes in v4:
time: 68.6 us; the launch traced here: 68.5 us
  Pallas kernels  67.2 us (98%)
  between operations  1.29 us (2%)
    pallas_call x1, Pallas kernels, shards(): pl.pallas_call(kernel, out_shape=[jax.ShapeDtypeStruct(s, F32) for s in O...  65.3 us
    pallas_call x1, Pallas kernels, shards(): pl.pallas_call(put_out, out_shape=[jax.ShapeDtypeStruct(s, F32) for s in...  1.87 us

profile of v4, /device:TPU:1, one launch (start us, length us, event | category | flops | bytes accessed | tf_op | source)
XLA Modules:
  0.0 68.5 jit_solution(12974170720681114923)
XLA Ops:
  1.3 65.3 %shard_map.145 = (f32[64,1024]{1,0:T(8,128)}, f32[1,1024]{1,0:T(1,128)}, f32[64,64]{1,0:T(8,128)}, f32[64,1024]{1,0:T(8,128)}, f32[1,64]{1,0:T(1,128)}, /*index=5*/f32[64,64]{1,0:T(8,128)}) custom-call(bf16[320,1024]{1,0:T(8,128)(2,1)} %bitcast.16, bf16[64,320]{1,0:T(8,128)(2,1)} %bitcast.18, f32[1,320]{1,0:T(1,128)} %bitcast.21, f32[1,320]{1,0:T(1,128)} %bitcast.22, ...), custom_call_target="tpu_custom_call" | custom-call | tf_op jit(solution)/shard_map/pallas_call | solution.py:550
  66.6 1.9 %shard_map.146 = (f32[64,1024]{1,0:T(8,128)}, f32[1,1024]{1,0:T(1,128)}, f32[64,64]{1,0:T(8,128)}, f32[64,1024]{1,0:T(8,128)}, f32[1,64]{1,0:T(1,128)}, /*index=5*/f32[64,64]{1,0:T(8,128)}) custom-call(f32[64,1024]{1,0:T(8,128)} %get-tuple-element.18.refs_0_, f32[1,1024]{1,0:T(1,128)} %get-tuple-element.19.refs_1_, f32[64,64]{1,0:T(8,128)} %get-tuple-element.20.refs_2_, ...), custom_call_target="tpu_custom_call" | custom-call | tf_op jit(solution)/shard_map/pallas_call | solution.py:618

commit v5 on v4

--- a/solution.py
+++ b/solution.py
@@ -12,6 +12,8 @@
 
 NX, NY, NZ = 4, 8, 8
 M, S, PS = 320, 64, 1024
+FAR8 = (4, 3, 5, 2, 6, 1, 7)
+FAR4 = (2, 1, 3)
 VMEM_ALL = 67043328
 OUTS = [(64, PS), (1, PS), (S, S), (S, PS), (1, S), (S, S)]
 
@@ -58,6 +60,12 @@
             src_ref=src, dst_ref=dst, send_sem=send, recv_sem=recv,
             device_id=dev, device_id_type=MESH,
         )
+
+    barrier = pltpu.get_barrier_semaphore()
+    partners = [dev(k) for k in FAR8 for dev in (y_dev, z_dev)]
+    partners += [x_dev(k) for k in FAR4] + [core_dev]
+    for dev in partners:
+        pl.semaphore_signal(barrier, inc=1, device_id=dev, device_id_type=MESH)
 
     loads = [
         pltpu.make_async_copy(a, b, in_s.at[i])
@@ -79,13 +87,6 @@
             ]
         )
     ]
-    barrier = pltpu.get_barrier_semaphore()
-    partners = [core_dev]
-    partners += [x_dev(k) for k in range(1, NX)]
-    partners += [y_dev(k) for k in range(1, NY)]
-    partners += [z_dev(k) for k in range(1, NZ)]
-    for dev in partners:
-        pl.semaphore_signal(barrier, inc=1, device_id=dev, device_id_type=MESH)
 
     rows = lax.broadcasted_iota(jnp.int32, (M, M), 0)
     lanes = lax.broadcasted_iota(jnp.int32, (M, M), 1)
@@ -100,7 +101,7 @@
     def tx(k):
         return copy(TX.at[x], TX.at[x], tx_s.at[k - 1], tx_r.at[k - 1], x_dev(k))
 
-    for k in range(1, NX):
+    for k in FAR4:
         tx(k).start()
 
     link = jnp.where(seg < NX * NY - 1, 1.0, 0.0).astype(F32)
@@ -128,7 +129,7 @@
     def ty(k):
         return copy(TY.at[y], TY.at[y], ty_s.at[k - 1], ty_r.at[k - 1], y_dev(k))
 
-    for k in range(1, NY):
+    for k in FAR8:
         ty(k).start()
 
     smap = jnp.dot(
@@ -266,7 +267,7 @@
     def gx(k):
         return copy(GX.at[x], GX.at[x], gx_s.at[k - 1], gx_r.at[k - 1], x_dev(k))
 
-    for k in range(1, NX):
+    for k in FAR4:
         gx(k).start()
 
     state_rows = weight_row * ss[...].astype(F32)
@@ -322,7 +323,7 @@
     def gy(k):
         return copy(GY.at[y], GY.at[y], gy_s.at[k - 1], gy_r.at[k - 1], y_dev(k))
 
-    for k in range(1, NY):
+    for k in FAR8:
         gy(k).start()
 
     x_last(0)
@@ -382,7 +383,7 @@
     def gz(k):
         return copy(GZ.at[z], GZ.at[z], gz_s.at[k - 1], gz_r.at[k - 1], z_dev(k))
 
-    for k in range(1, NZ):
+    for k in FAR8:
         gz(k).start()
 
     @pl.when(last_x & (y > 0))
@@ -396,7 +397,7 @@
         for d in range(2):
             pn(g, d).wait_recv()
         V[g] = W[g, lines[g][0]] + R1[g, 0, 3] + R1[g, 1, 3]
-        for k in range(1, 8):
+        for k in FAR8:
             qc(g, k).start()
     for k in range(1, NZ):
         gz(k).wait_recv()
@@ -407,32 +408,37 @@
     grad[...] = part * scale
     results[1].start()
 
-    done = []
+    def ay(g, k):
+        block = FA.at[x, y] if g == 0 else FB.at[y]
+        return copy(block, block, ay_s.at[g, k - 1], ay_r.at[g, k - 1], y_dev(k))
+
+    def ax(g, k):
+        block = FA.at[x] if g == 0 else FB.at[y, x]
+        return copy(block, block, ax_s.at[g, k - 1], ax_r.at[g, k - 1], x_dev(k))
+
     for g in range(2):
         own = V[g, lines[g][2]]
         for k in range(1, 8):
             qc(g, k).wait_recv()
             own = own + R2[g, k - 1]
-        done.append(own * scale)
-    FA[x, y] = done[0]
-    FB[y, x] = done[1]
-
-    def ay(g, k):
-        block = FA.at[x, y] if g == 0 else FB.at[y]
-        return copy(block, block, ay_s.at[g, k - 1], ay_r.at[g, k - 1], y_dev(k))
-
-    def ax(g, k):
-        block = FA.at[x] if g == 0 else FB.at[y, x]
-        return copy(block, block, ax_s.at[g, k - 1], ax_r.at[g, k - 1], x_dev(k))
-
-    for k in range(1, NY):
-        ay(0, k).start()
-    for k in range(1, NX):
-        ax(1, k).start()
+        if g == 0:
+            FA[x, y] = own * scale
+            for k in FAR8:
+                ay(0, k).start()
+        else:
+            FB[y, x] = own * scale
+            for k in FAR4:
+                ax(1, k).start()
+
     for k in range(1, NX):
         ax(1, k).wait_recv()
+    for k in FAR8:
+        ay(1, k).start()
+
     for k in range(1, NY):
-        ay(1, k).start()
+        ay(0, k).wait_recv()
+    for k in FAR4:
+        ax(0, k).start()
 
     @pl.when(seg > 0)
     def _():
@@ -445,22 +451,18 @@
     for i in (2, 3, 4):
         results[i].start()
 
-    for k in range(1, NY):
-        ay(0, k).wait_recv()
-    for k in range(1, NX):
-        ax(0, k).start()
-    for k in range(1, NY):
-        ay(1, k).wait_recv()
-    for k in range(1, NX):
-        ax(0, k).wait_recv()
-
     mine, theirs = pl.ds(4 * c, 4), pl.ds(4 * (1 - c), 4)
     swap = [
         copy(FA.at[:, theirs], FAr, fin_s.at[0], fin_r.at[0], core_dev),
         copy(FB.at[theirs], FBr, fin_s.at[1], fin_r.at[1], core_dev),
     ]
-    for one in swap:
-        one.start()
+    for k in range(1, NY):
+        ay(1, k).wait_recv()
+    swap[1].start()
+    for k in range(1, NX):
+        ax(0, k).wait_recv()
+
+    swap[0].start()
 
     def place(owner, first, second):
         at = pl.multiple_of(((owner + NZ - z) % NZ) * 128, 128)

time: 68.6 us -> 68 us (level)
  Pallas kernels: 67.2 us -> 66.5 us
where the time goes in v5:
time: 68 us; the launch traced here: 67.8 us
  Pallas kernels  66.5 us (98%)
  between operations  1.29 us (2%)
    pallas_call x1, Pallas kernels, shards(): pl.pallas_call(kernel, out_shape=[jax.ShapeDtypeStruct(s, F32) for s in O...  64.7 us
    pallas_call x1, Pallas kernels, shards(): pl.pallas_call(put_out, out_shape=[jax.ShapeDtypeStruct(s, F32) for s in...  1.87 us

profile of v5, /device:TPU:1, one launch (start us, length us, event | category | flops | bytes accessed | tf_op | source)
XLA Modules:
  0.0 67.8 jit_solution(901764080450279049)
XLA Ops:
  1.3 64.7 %shard_map.145 = (f32[64,1024]{1,0:T(8,128)}, f32[1,1024]{1,0:T(1,128)}, f32[64,64]{1,0:T(8,128)}, f32[64,1024]{1,0:T(8,128)}, f32[1,64]{1,0:T(1,128)}, /*index=5*/f32[64,64]{1,0:T(8,128)}) custom-call(bf16[320,1024]{1,0:T(8,128)(2,1)} %bitcast.16, bf16[64,320]{1,0:T(8,128)(2,1)} %bitcast.18, f32[1,320]{1,0:T(1,128)} %bitcast.21, f32[1,320]{1,0:T(1,128)} %bitcast.22, ...), custom_call_target="tpu_custom_call" | custom-call | tf_op jit(solution)/shard_map/pallas_call | solution.py:552
  66.0 1.9 %shard_map.146 = (f32[64,1024]{1,0:T(8,128)}, f32[1,1024]{1,0:T(1,128)}, f32[64,64]{1,0:T(8,128)}, f32[64,1024]{1,0:T(8,128)}, f32[1,64]{1,0:T(1,128)}, /*index=5*/f32[64,64]{1,0:T(8,128)}) custom-call(f32[64,1024]{1,0:T(8,128)} %get-tuple-element.18.refs_0_, f32[1,1024]{1,0:T(1,128)} %get-tuple-element.19.refs_1_, f32[64,64]{1,0:T(8,128)} %get-tuple-element.20.refs_2_, ...), custom_call_target="tpu_custom_call" | custom-call | tf_op jit(solution)/shard_map/pallas_call | solution.py:620

commit v6 on v5

--- a/solution.py
+++ b/solution.py
@@ -281,9 +281,6 @@
     HB[...] = jnp.zeros_like(HB)
     HB[0:S, 0:S] = pgram[S:, S:] + small[S:, S:]
     HB[S : S + 1, 0:S] = pgrad[:, S:] + state_grad[:, S:]
-    cross[...] = pcross[:S] + wide[:S]
-    hess[...] = pgram[:S, :S] + small[:S, :S]
-    ngrad[...] = pgrad[:, :S] - state_grad[:, :S]
 
 
     pass_halo = [
@@ -315,6 +312,10 @@
     def _():
         for h in halo:
             h.start()
+
+    cross[...] = pcross[:S] + wide[:S]
+    hess[...] = pgram[:S, :S] + small[:S, :S]
+    ngrad[...] = pgrad[:, :S] - state_grad[:, :S]
 
     for k in range(1, NX):
         gx(k).wait_recv()

time: 68 us -> 68 us (level)
  no operation moved by 1% of the time
where the time goes in v6:
time: 68 us; the launch traced here: 67.8 us
  Pallas kernels  66.5 us (98%)
  between operations  1.29 us (2%)
    pallas_call x1, Pallas kernels, shards(): pl.pallas_call(kernel, out_shape=[jax.ShapeDtypeStruct(s, F32) for s in O...  64.7 us
    pallas_call x1, Pallas kernels, shards(): pl.pallas_call(put_out, out_shape=[jax.ShapeDtypeStruct(s, F32) for s in...  1.87 us

profile of v6, /device:TPU:1, one launch (start us, length us, event | category | flops | bytes accessed | tf_op | source)
XLA Modules:
  0.0 67.8 jit_solution(8058847874012660889)
XLA Ops:
  1.3 64.7 %shard_map.145 = (f32[64,1024]{1,0:T(8,128)}, f32[1,1024]{1,0:T(1,128)}, f32[64,64]{1,0:T(8,128)}, f32[64,1024]{1,0:T(8,128)}, f32[1,64]{1,0:T(1,128)}, /*index=5*/f32[64,64]{1,0:T(8,128)}) custom-call(bf16[320,1024]{1,0:T(8,128)(2,1)} %bitcast.16, bf16[64,320]{1,0:T(8,128)(2,1)} %bitcast.18, f32[1,320]{1,0:T(1,128)} %bitcast.21, f32[1,320]{1,0:T(1,128)} %bitcast.22, ...), custom_call_target="tpu_custom_call" | custom-call | tf_op jit(solution)/shard_map/pallas_call | solution.py:553
  66.0 1.9 %shard_map.146 = (f32[64,1024]{1,0:T(8,128)}, f32[1,1024]{1,0:T(1,128)}, f32[64,64]{1,0:T(8,128)}, f32[64,1024]{1,0:T(8,128)}, f32[1,64]{1,0:T(1,128)}, /*index=5*/f32[64,64]{1,0:T(8,128)}) custom-call(f32[64,1024]{1,0:T(8,128)} %get-tuple-element.18.refs_0_, f32[1,1024]{1,0:T(1,128)} %get-tuple-element.19.refs_1_, f32[64,64]{1,0:T(8,128)} %get-tuple-element.20.refs_2_, ...), custom_call_target="tpu_custom_call" | custom-call | tf_op jit(solution)/shard_map/pallas_call | solution.py:621
